TPU v7x, 512 devices: a whole 4x4x16 slice. The times are simulated.
512 devices in a mesh: row: 32 (over z, y_lo), col: 16 (over x, y_hi, core).
Axes of the slice: x: 4, y: 4 (y_hi: 2, y_lo: 2; y = y_hi * 2 + y_lo), z: 16, core: 2. Of those that a mesh axis runs over, the one named last changes fastest.
Arguments:
- pair_in: bfloat16 [384, 384, 128], P('row', 'col'), may hold values from -6 to 6
- cotangent: bfloat16 [384, 384, 128], P('row', 'col'), may hold values from -6 to 6
- in_gain: float32 [128], replicated, may hold values from 0.25 to 1.75
- in_bias: float32 [128], replicated, may hold values from -3 to 3
- in_weights: bfloat16 [128, 640], replicated, may hold values from -0.5 to 0.5
- out_gain: float32 [128], replicated, may hold values from 0.25 to 1.75
- out_bias: float32 [128], replicated, may hold values from -3 to 3
- out_weights: bfloat16 [128, 128], replicated, may hold values from -0.5 to 0.5
Outputs:
- pair_out: bfloat16 [384, 384, 128], P('row', 'col')
- grad_pair: bfloat16 [384, 384, 128], P('row', 'col')
- grad_in_weights: float32 [128, 640], replicated
- grad_out_weights: float32 [128, 128], replicated
- grad_norms: float32 [4, 128], replicated
All inputs are finite; a program needn't handle non-finite values.
Results may differ from a plain program's by a relative error of at most 0.015.
Values may be sent and summed in bfloat16 or wider, within the bound.
No kernel may reach another device: no remote copies, remote signals or barrier semaphores. Data moves between devices by JAX's collectives and lax.ppermute only.
A program may use at most 64 MiB of HBM per device.

v0:
```python
import jax
import jax.numpy as jnp
from jax import lax
from jax.sharding import PartitionSpec as P


def layer_stats(values):
    average = jnp.mean(values, axis=-1, keepdims=True)
    centred = values - average
    inv_std = lax.rsqrt(jnp.mean(centred * centred, axis=-1, keepdims=True) + 1e-05)
    return (centred * inv_std, inv_std)


def layer_back(upstream, normal_hat, inv_std, scaling):
    scaled = upstream * scaling
    bracket = (
        scaled
        - jnp.mean(scaled, axis=-1, keepdims=True)
        - normal_hat * jnp.mean(scaled * normal_hat, axis=-1, keepdims=True)
    )
    return inv_std * bracket


def local(pair_in, cotangent, in_gain, in_bias, in_weights, out_gain, out_bias, out_weights):
    channels = pair_in.shape[2]
    in_hat, in_rstd = layer_stats(pair_in.astype(jnp.float32))
    in_norm = (in_hat * in_gain + in_bias).astype(jnp.bfloat16)
    projected = jnp.einsum("ijc,cd->ijd", in_norm, in_weights, preferred_element_type=jnp.float32)
    lin_left = projected[:, :, :channels]
    left_sig = jax.nn.sigmoid(projected[:, :, channels : 2 * channels])
    lin_right = projected[:, :, 2 * channels : 3 * channels]
    right_sig = jax.nn.sigmoid(projected[:, :, 3 * channels : 4 * channels])
    gate_act = jax.nn.sigmoid(projected[:, :, 4 * channels :])
    left_act = (left_sig * lin_left).astype(jnp.bfloat16)
    right_act = (right_sig * lin_right).astype(jnp.bfloat16)
    left_panel = lax.all_gather(left_act, "col", axis=1, tiled=True)
    right_cols = lax.all_gather(right_act, "row", axis=0, tiled=True)
    right_panel = lax.all_to_all(right_cols, "col", split_axis=0, concat_axis=1, tiled=True)
    product = jnp.einsum(
        "ikc,jkc->ijc", left_panel, right_panel, preferred_element_type=jnp.float32
    )
    out_hat, out_rstd = layer_stats(product)
    out_norm = (out_hat * out_gain + out_bias).astype(jnp.bfloat16)
    out_lin = jnp.einsum("ijc,cd->ijd", out_norm, out_weights, preferred_element_type=jnp.float32)
    pair_out = (gate_act * out_lin).astype(jnp.bfloat16)
    upstream = cotangent.astype(jnp.float32)
    d_lin = (upstream * gate_act).astype(jnp.bfloat16)
    d_gate = upstream * out_lin
    d_outnorm = jnp.einsum("ijd,cd->ijc", d_lin, out_weights, preferred_element_type=jnp.float32)
    d_product = layer_back(d_outnorm, out_hat, out_rstd, out_gain).astype(jnp.bfloat16)
    left_terms = jnp.einsum(
        "ijc,jkc->ikc", d_product, right_panel, preferred_element_type=jnp.float32
    )
    d_left = lax.psum_scatter(
        left_terms.astype(jnp.bfloat16), "col", scatter_dimension=1, tiled=True
    ).astype(jnp.float32)
    right_terms = jnp.einsum(
        "ijc,ikc->jkc", d_product, left_panel, preferred_element_type=jnp.float32
    ).astype(jnp.bfloat16)
    right_back = lax.all_to_all(right_terms, "col", split_axis=1, concat_axis=0, tiled=True)
    d_right = lax.psum_scatter(
        right_back.astype(jnp.float32).astype(jnp.bfloat16), "row", scatter_dimension=0, tiled=True
    ).astype(jnp.float32)
    d_proj = jnp.concatenate(
        [
            d_left * left_sig,
            d_left * lin_left * left_sig * (1.0 - left_sig),
            d_right * right_sig,
            d_right * lin_right * right_sig * (1.0 - right_sig),
            d_gate * gate_act * (1.0 - gate_act),
        ],
        axis=-1,
    ).astype(jnp.bfloat16)
    d_innorm = jnp.einsum("ijd,cd->ijc", d_proj, in_weights, preferred_element_type=jnp.float32)
    grad_pair = layer_back(d_innorm, in_hat, in_rstd, in_gain).astype(jnp.bfloat16)
    local_in = jnp.einsum("ijc,ijd->cd", in_norm, d_proj, preferred_element_type=jnp.float32)
    local_out = jnp.einsum("ijc,ijd->cd", out_norm, d_lin, preferred_element_type=jnp.float32)
    local_norms = jnp.stack(
        [
            jnp.sum(d_innorm * in_hat, axis=(0, 1)),
            jnp.sum(d_innorm, axis=(0, 1)),
            jnp.sum(d_outnorm * out_hat, axis=(0, 1)),
            jnp.sum(d_outnorm, axis=(0, 1)),
        ]
    )
    summed_in, summed_out, summed_norms = lax.psum(
        (local_in, local_out, local_norms), ("row", "col")
    )
    per_residue = 1.0 / left_panel.shape[1]
    return (
        pair_out,
        grad_pair,
        summed_in * per_residue,
        summed_out * per_residue,
        summed_norms * per_residue,
    )


def solution(mesh):
    return jax.shard_map(
        local,
        mesh=mesh,
        in_specs=(P("row", "col", None), P("row", "col", None), P(), P(), P(), P(), P(), P()),
        out_specs=(P("row", "col", None), P("row", "col", None), P(), P(), P()),
        check_vma=False,
    )
```

profile of v0, /device:TPU:1, one launch (start us, length us, event | category | flops | bytes accessed | tf_op | source)
XLA Modules:
  0.0 1074.1 jit_solution(5752170956004256796)
XLA Ops:
  7.2 1.0 convert_reduce_fusion
  8.3 1.1 fusion.18
  9.4 1.3 fusion.9
  12.2 117.9 %all-gather.3.cloned.1.call-done = bf16[384,24,128]{2,1,0:T(8,128)(2,1)} async-done(((bf16[12,24,128]{2,1,0:T(8,128)(2,1)}), bf16[384,24,128]{2,1,0:T(8,128)(2,1)}) %all-gather.3.cloned.1.call-update) | async-done | bytes 2359312 | tf_op jit(solution)/shard_map/all_gather | solution.py:37
  130.1 28.3 %all-to-all-start = ((bf16[384,24,128]{2,1,0:T(8,128)(2,1)}), bf16[384,24,128]{2,1,0:T(8,128)(2,1)S(1)}, u32[]{:S(2)}, u32[]{:S(2)}) async-start(bf16[384,24,128]{2,1,0:T(8,128)(2,1)} %all-gather.3.cloned.1.call-done), calls=%async_computation | async-start | bytes 4718592 | tf_op jit(solution)/shard_map/all_to_all | solution.py:38
  158.4 61.3 %all-gather.5.cloned.1.call-done = bf16[12,384,128]{2,1,0:T(8,128)(2,1)} async-done(((bf16[12,24,128]{2,1,0:T(8,128)(2,1)}), bf16[12,384,128]{2,1,0:T(8,128)(2,1)}) %all-gather.5.cloned.1.call-update) | async-done | bytes 1179664 | tf_op jit(solution)/shard_map/all_gather | solution.py:36
  219.7 2.9 copy.74
  222.6 2.0 copy.72
  224.7 3.3 copy.73
  228.0 3.5 fusion.56
  231.4 1.5 copy.75
  233.3 1.1 multiply_reduce_fusion
  234.6 1.2 copy.77
  235.9 4.0 convert_bitcast_fusion
  239.8 4.7 copy.81
  244.5 4.5 all-to-all-start.1
  249.0 2.8 fusion
  251.8 2.6 copy.85
  254.4 1.4 copy.92
  255.9 24.4 %all-to-all-done.1 = bf16[24,384,128]{2,0,1:T(8,128)(2,1)} async-done(((bf16[24,384,128]{2,0,1:T(8,128)(2,1)}), bf16[24,384,128]{2,0,1:T(8,128)(2,1)}, u32[]{:S(2)}, u32[]{:S(2)}) %all-to-all-start.1) | async-done | bytes 2359328 | tf_op jit(solution)/shard_map/all_to_all | solution.py:60
  280.2 3.6 copy.83
  284.7 1.0 convolution_bitcast_fusion.1
  286.6 59.3 %reduce-scatter.7.cloned.1.call-done = bf16[24,1536]{1,0:T(8,128)(2,1)} async-done(((bf16[384,1536]{1,0:T(8,128)(2,1)}), bf16[24,1536]{1,0:T(8,128)(2,1)}) %reduce-scatter.7.cloned.1.call-update) | async-done | bytes 73744
  345.9 1.0 reshape.59
  347.0 121.3 %reduce-scatter.5.cloned.1.call-done = bf16[12,24,128]{2,1,0:T(8,128)(2,1)} async-done(((bf16[384,24,128]{2,1,0:T(8,128)(2,1)}), bf16[12,24,128]{2,1,0:T(8,128)(2,1)}) %reduce-scatter.5.cloned.1.call-update) | async-done | bytes 73744 | tf_op jit(solution)/shard_map/reduce_scatter | solution.py:61
  468.3 0.9 fusion.42
  469.2 1.0 fusion.41
  470.7 1.1 convolution_bitcast_fusion
  471.8 123.6 %psum.23 = f32[4,128]{1,0:T(4,128)S(1)} all-reduce(f32[4,128]{1,0:T(4,128)S(1)} %pad_maximum_fusion), channel_id=1, replica_groups=mesh['row'=32,'col'=16] {'row','col'}, use_global_device_ids=true, to_apply=%region_16.0 | all-reduce | flops 512 | bytes 4096 | tf_op jit(solution)/shard_map/psum | solution.py:86
  596.8 467.6 %all-reduce.3.cloned.1.call-done = (f32[128,640]{1,0:T(8,128)}, f32[128,128]{1,0:T(8,128)}) async-done(((f32[128,640]{1,0:T(8,128)}, f32[128,128]{1,0:T(8,128)}), (f32[128,640]{1,0:T(8,128)}, f32[128,128]{1,0:T(8,128)})) %all-reduce.3.cloned.1.call-update) | async-done | bytes 393232 | tf_op jit(solution)/shard_map/psum | solution.py:86
  1064.4 1.7 broadcast_multiply_fusion
  1066.1 1.5 broadcast_multiply_fusion.1
  (48 shorter events, 6.0 us)
Async XLA Ops:
  7.2 2.2 copy-start
  7.2 122.9 %all-gather.3.cloned.1.call-start = ((), (), s32[]{:S(2)}) async-start(), calls=%async_computation.4 | async-start | bytes 2433024 | tf_op jit(solution)/shard_map/all_gather | solution.py:37
  11.4 208.3 %all-gather.5.cloned.1.call-start = ((), (), s32[]{:S(2)}) async-start(), calls=%async_computation.5 | async-start | bytes 1253376 | tf_op jit(solution)/shard_map/all_gather | solution.py:36
  130.1 92.5 %all-to-all-start = ((bf16[384,24,128]{2,1,0:T(8,128)(2,1)}), bf16[384,24,128]{2,1,0:T(8,128)(2,1)S(1)}, u32[]{:S(2)}, u32[]{:S(2)}) async-start(bf16[384,24,128]{2,1,0:T(8,128)(2,1)} %all-gather.3.cloned.1.call-done), calls=%async_computation | async-start | bytes 4718592 | tf_op jit(solution)/shard_map/all_to_all | solution.py:38
  228.0 5.3 copy-start.2
  228.0 5.3 copy-start.6
  244.5 35.8 %all-to-all-start.1 = ((bf16[24,384,128]{2,0,1:T(8,128)(2,1)}), bf16[24,384,128]{2,0,1:T(8,128)(2,1)}, u32[]{:S(2)}, u32[]{:S(2)}) async-start(bf16[24,384,128]{2,0,1:T(8,128)(2,1)} %copy.81), calls=%async_computation.1 | async-start | bytes 4718592 | tf_op jit(solution)/shard_map/all_to_all | solution.py:60
  248.9 97.0 %reduce-scatter.7.cloned.1.call-start = ((), (), s32[]{:S(2)}) async-start(), calls=%async_computation.7 | async-start | bytes 1253376
  255.8 212.5 %reduce-scatter.5.cloned.1.call-start = ((), (), s32[]{:S(2)}) async-start(), calls=%async_computation.6 | async-start | bytes 2433024 | tf_op jit(solution)/shard_map/reduce_scatter | solution.py:61
  283.8 0.9 copy-start.3
  283.8 0.9 copy-start.8
  283.8 1.9 copy-start.7
  283.8 186.4 %copy-start.1 = (bf16[12,24,128]{2,1,0:T(8,128)(2,1)S(1)}, bf16[12,24,128]{2,1,0:T(8,128)(2,1)}, u32[]{:S(2)}) copy-start(bf16[12,24,128]{2,1,0:T(8,128)(2,1)} %param.8) | copy-start | bytes 221188
  283.9 186.4 %copy-start.4 = (f32[128]{0:T(128)S(1)}, f32[128]{0:T(128)}, u32[]{:S(2)}) copy-start(f32[128]{0:T(128)} %param.10) | copy-start | bytes 1540
  283.9 186.8 %copy-start.5 = (f32[128]{0:T(128)S(1)}, f32[128]{0:T(128)}, u32[]{:S(2)}) copy-start(f32[128]{0:T(128)} %param.11) | copy-start | bytes 1540
  283.9 780.5 %all-reduce.3.cloned.1.call-start = ((), (), s32[]{:S(2)}) async-start(), calls=%async_computation.8 | async-start | bytes 786432 | tf_op jit(solution)/shard_map/psum | solution.py:86
Sparse Core Ops, SparseCore 0:
  11.5 118.5 all-gather.2
  133.8 85.8 all-gather.4
  255.9 89.8 reduce-scatter.6
  348.6 119.6 reduce-scatter.4
  595.5 468.8 all-reduce.2
where the time goes:
time: 1080 us; the launch traced here: 1070 us
  waiting for transfers between devices  853 us (79%)
  blocking collectives  124 us (11%)
  starting transfers between devices  32.9 us (3%)
  local copies, waits for them, and re-layouts  25 us (2%)
  matrix products  16 us (1%)
  between operations  14 us (1%)
    psum x1, waiting for transfers between devices, local(): lax.psum((local_in, local_out, local_norms), ('row', 'col'))  468 us
    psum x1, blocking collectives, local(): lax.psum((local_in, local_out, local_norms), ('row', 'col'))  124 us
    reduce_scatter x1, waiting for transfers between devices, local(): lax.psum_scatter(right_back.astype(jnp.float32).astype(jnp.bfloat16), 'ro...  121 us
    all_gather x1, waiting for transfers between devices, local(): right_cols = lax.all_gather(right_act, 'row', axis=0, tiled=True)  118 us
    all_gather x1, waiting for transfers between devices, local(): left_panel = lax.all_gather(left_act, 'col', axis=1, tiled=True)  61.3 us
    unnamed x6, waiting for transfers between devices  60.1 us
    all_to_all x1, starting transfers between devices, local(): lax.all_to_all(right_cols, 'col', split_axis=0, concat_axis=1, tiled=True)  28.3 us
    all_to_all x1, waiting for transfers between devices, local(): lax.all_to_all(right_terms, 'col', split_axis=1, concat_axis=0, tiled=True)  24.4 us
  transfers between devices with their start and end apart: 7, of which 6 were waited for; matrix products, arithmetic and copies ran while one was open for 2% of the time, Pallas kernels for 0%

commit v1 on v0

v1 whole, which is shorter than its diff:
```python
import jax
import jax.numpy as jnp
from jax import lax
from jax.sharding import Mesh, PartitionSpec as P

GROUP = ("rr", "col")
BF = jnp.bfloat16
F32 = jnp.float32


def dot(a, b, da, db):
    return lax.dot_general(a, b, (((da,), (db,)), ((), ())), preferred_element_type=F32)


def stats(values, axis):
    average = jnp.mean(values, axis=axis, keepdims=True)
    centred = values - average
    inv_std = lax.rsqrt(jnp.mean(centred * centred, axis=axis, keepdims=True) + 1e-05)
    return centred * inv_std, inv_std


def back(upstream, hat, inv_std, scaling, axis):
    scaled = upstream * scaling
    return inv_std * (
        scaled
        - jnp.mean(scaled, axis=axis, keepdims=True)
        - hat * jnp.mean(scaled * hat, axis=axis, keepdims=True)
    )


def exchange(x):
    return lax.all_to_all(x, GROUP, split_axis=0, concat_axis=0, tiled=True)


def local(pair_in, cotangent, in_gain, in_bias, in_weights, out_gain, out_bias, out_weights):
    ni, nk, c = pair_in.shape
    rr, cols, rq = lax.axis_size("rr"), lax.axis_size("col"), lax.axis_size("rq")
    pairs = ni * nk
    rows, all_k = rr * ni, cols * nk

    def to_matrix(x):
        x = x.reshape(rr, cols, -1, ni, nk).transpose(2, 0, 3, 1, 4)
        return x.reshape(-1, rows, all_k)

    def from_matrix(x):
        x = x.reshape(-1, rr, ni, cols, nk).transpose(1, 3, 0, 2, 4)
        return x.reshape(c, -1)

    in_hat, in_rstd = stats(pair_in.reshape(pairs, c).astype(F32), 1)
    in_norm = (in_hat * in_gain + in_bias).astype(BF)
    w_gate = in_weights[:, 4 * c :]
    proj = dot(in_weights[:, : 4 * c], in_norm, 0, 1)
    gate = jax.nn.sigmoid(dot(in_norm, w_gate, 1, 0))
    lin_left, lin_right = proj[:c], proj[2 * c : 3 * c]
    left_sig = jax.nn.sigmoid(proj[c : 2 * c])
    right_sig = jax.nn.sigmoid(proj[3 * c :])
    left = (left_sig * lin_left).astype(BF)
    right = (right_sig * lin_right).astype(BF)

    got = exchange(jnp.concatenate([left, right], axis=1))
    mats = to_matrix(got)
    gathered = lax.all_gather(mats, "rq")
    left_all = gathered[:, 0].reshape(rq * rows, all_k)
    right_all = gathered[:, 1].reshape(rq * rows, all_k)
    product = dot(mats[0], right_all, 1, 1)
    prod = exchange(from_matrix(product))

    out_hat, out_rstd = stats(prod, 0)
    gain_col = out_gain[:, None]
    out_norm = (out_hat * gain_col + out_bias[:, None]).astype(BF)
    out_lin = dot(out_norm, out_weights, 0, 0)
    pair_out = (gate * out_lin).astype(BF)
    upstream = cotangent.reshape(pairs, c).astype(F32)
    d_lin = (upstream * gate).astype(BF)
    d_gate = upstream * out_lin
    d_outnorm = dot(out_weights, d_lin, 1, 1)
    d_product = back(d_outnorm, out_hat, out_rstd, gain_col, 0).astype(BF)

    d_mat = to_matrix(exchange(d_product))[0]
    d_all = lax.all_gather(d_mat, "rq").reshape(rq * rows, all_k)
    d_left_m = dot(d_mat, right_all, 1, 0).astype(BF)
    d_right_m = dot(d_all, left_all, 0, 0).astype(BF)
    d_right_m = lax.dynamic_slice_in_dim(d_right_m, lax.axis_index("rq") * rows, rows, 0)
    d_both = exchange(from_matrix(jnp.stack([d_left_m, d_right_m]))).astype(F32)
    d_left, d_right = d_both[:, :pairs], d_both[:, pairs:]

    d_proj = [
        (d_left * left_sig).astype(BF),
        (d_left * lin_left * left_sig * (1.0 - left_sig)).astype(BF),
        (d_right * right_sig).astype(BF),
        (d_right * lin_right * right_sig * (1.0 - right_sig)).astype(BF),
    ]
    d_five = (d_gate * gate * (1.0 - gate)).astype(BF)
    d_innorm = dot(jnp.concatenate(d_proj), in_weights[:, : 4 * c], 0, 1) + dot(d_five, w_gate, 1, 1)
    grad_pair = back(d_innorm, in_hat, in_rstd, in_gain, 1).astype(BF)

    norms = jnp.stack(
        [
            jnp.sum(d_innorm * in_hat, axis=0),
            jnp.sum(d_innorm, axis=0),
            jnp.sum(d_outnorm * out_hat, axis=1),
            jnp.sum(d_outnorm, axis=1),
        ]
    )
    blocks = [dot(in_norm, part, 0, 1) for part in d_proj]
    blocks += [dot(in_norm, d_five, 0, 0), dot(out_norm, d_lin, 1, 0), norms]
    used = 6 * c + 4
    slots = 8 * c
    stacked = jnp.concatenate(blocks + [jnp.zeros((slots - used, c), F32)])
    mine = jnp.sum(exchange(stacked.reshape(c, 8, c)), axis=0)
    quarter = lax.all_gather(mine, "rq")
    total = (quarter[0] + quarter[1]) + (quarter[2] + quarter[3])
    total = total * (1.0 / all_k)
    summed = exchange(jnp.broadcast_to(total[None], (c, 8, c))).reshape(slots, c)
    grad_in = jnp.concatenate([summed[b * c : (b + 1) * c] for b in range(5)], axis=1)
    return (
        pair_out.reshape(ni, nk, c),
        grad_pair.reshape(ni, nk, c),
        grad_in,
        summed[5 * c : 6 * c],
        summed[6 * c : used],
    )


def solution(mesh):
    grid = mesh.devices.reshape(4, mesh.devices.shape[0] // 4, mesh.devices.shape[1])
    split = Mesh(grid, ("rq", "rr", "col"))
    pair = P(("rq", "rr"), "col", None)
    return jax.shard_map(
        local,
        mesh=split,
        in_specs=(pair, pair, P(), P(), P(), P(), P(), P()),
        out_specs=(pair, pair, P(), P(), P()),
        check_vma=False,
    )
```

time: 1080 us -> 230 us (0.21)
  waiting for transfers between devices: 853 us -> 39.2 us
  between operations: 14 us -> 1.17 us
  blocking collectives: 124 us -> 136 us
  matrix products: 16 us -> 4.47 us
  starting transfers between devices: 32.9 us -> 21.4 us
    psum x1 -> x0, waiting for transfers between devices: 468 us -> none  [local(): lax.psum((local_in, local_out, local_norms), ('row', 'col'))]
    all_gather x2 -> x0, waiting for transfers between devices: 179 us -> none  [the longest x1 118 us: local(): right_cols = lax.all_gather(right_act, 'row', axis=0, tiled=True)]
    psum x1 -> x0, blocking collectives: 124 us -> none  [local(): lax.psum((local_in, local_out, local_norms), ('row', 'col'))]
    reduce_scatter x1 -> x0, waiting for transfers between devices: 121 us -> none  [local(): lax.psum_scatter(right_back.astype(jnp.float32).astype(jnp.bfloat16), 'ro...]
    all_gather x0 -> x3, blocking collectives: none -> 69.6 us  [the longest x1 34.5 us: local(): gathered = lax.all_gather(mats, 'rq')]
    all_to_all x0 -> x3, blocking collectives: none -> 66.7 us  [exchange(): return lax.all_to_all(x, GROUP, split_axis=0, concat_axis=0, tiled=True)]
    unnamed x6 -> x0, waiting for transfers between devices: 60.1 us -> none
    all_to_all x2 -> x3, waiting for transfers between devices: 24.4 us -> 39.2 us  [exchange(): return lax.all_to_all(x, GROUP, split_axis=0, concat_axis=0, tiled=True)]
  transfers between devices with their start and end apart: 7 -> 3, of which waited for: 6 -> 3; matrix products, arithmetic and copies ran while one was open for 2% -> 1% of each run, Pallas kernels for 0% -> 0%
where the time goes in v1:
time: 230 us; the launch traced here: 229 us
  blocking collectives  136 us (59%)
  waiting for transfers between devices  39.2 us (17%)
  starting transfers between devices  21.4 us (9%)
  local copies, waits for them, and re-layouts  17.6 us (8%)
  other arithmetic  9.01 us (4%)
  matrix products  4.47 us (2%)
    all_to_all x3, blocking collectives, exchange(): return lax.all_to_all(x, GROUP, split_axis=0, concat_axis=0, tiled=True)  66.7 us
    all_to_all x3, waiting for transfers between devices, exchange(): return lax.all_to_all(x, GROUP, split_axis=0, concat_axis=0, tiled=True)  39.2 us
    all_gather x1, blocking collectives, local(): gathered = lax.all_gather(mats, 'rq')  34.5 us
    all_to_all x3, starting transfers between devices, exchange(): return lax.all_to_all(x, GROUP, split_axis=0, concat_axis=0, tiled=True)  21.4 us
    all_gather x1, blocking collectives, local(): d_all = lax.all_gather(d_mat, 'rq').reshape(rq * rows, all_k)  20.6 us
    all_gather x1, blocking collectives, local(): quarter = lax.all_gather(mine, 'rq')  14.5 us
    unnamed x34, local copies, waits for them, and re-layouts  6.22 us
    all_to_all x7, other arithmetic, exchange(): return lax.all_to_all(x, GROUP, split_axis=0, concat_axis=0, tiled=True)  4.92 us
  transfers between devices with their start and end apart: 3, of which 3 were waited for; matrix products, arithmetic and copies ran while one was open for 1% of the time, Pallas kernels for 0%

profile of v1, /device:TPU:1, one launch (start us, length us, event | category | flops | bytes accessed | tf_op | source)
XLA Modules:
  0.0 229.1 jit_solution(3491511967572022648)
XLA Ops:
  0.7 1.1 convert_reduce_fusion
  2.6 0.8 fusion.21
  4.3 0.7 reduce.6
  5.3 25.3 %all_to_all.51 = bf16[128,2,288]{2,1,0:T(2,128)(2,1)S(1)} all-to-all(bf16[128,2,288]{2,1,0:T(2,128)(2,1)S(1)} %reshape.169), channel_id=1, replica_groups=mesh['rq'=4,'rr'=8,'col'=16] {'rr','col'}, dimensions={0} | all-to-all | bytes 294912 | tf_op jit(solution)/shard_map/all_to_all | solution.py:32
  31.0 1.0 reduce.4
  32.0 1.5 reshape.141
  33.9 0.8 all_gather_reshape.3
  34.7 34.5 %all_gather.12 = bf16[4,2,96,384]{3,2,1,0:T(8,128)(2,1)S(1)} all-gather(bf16[1,2,96,384]{3,2,1,0:T(8,128)(2,1)S(1)} %all_gather_reshape.3), channel_id=1, replica_groups=mesh['rq'=4,'rr'=8,'col'=16] {'rq'}, dimensions={0}, use_global_device_ids=true | all-gather | bytes 737280 | tf_op jit(solution)/shard_map/all_gather | solution.py:62
  70.3 0.6 all_to_all.43
  70.9 17.7 %all_to_all.52 = f32[128,1,288]{2,1,0:T(1,128)S(1)} all-to-all(f32[128,1,288]{2,1,0:T(1,128)S(1)} %all_to_all.43), channel_id=1, replica_groups=mesh['rq'=4,'rr'=8,'col'=16] {'rr','col'}, dimensions={0} | all-to-all | bytes 294912 | tf_op jit(solution)/shard_map/all_to_all | solution.py:32
  89.2 0.6 copy-done.6
  90.2 0.7 copy-done.3
  91.0 0.9 fusion.13
  92.4 0.7 reduce.7
  93.2 0.8 reshape.171
  94.0 6.0 %all-to-all-start.2 = ((bf16[128,2,144]{2,1,0:T(2,128)(2,1)}), bf16[128,2,144]{2,1,0:T(2,128)(2,1)S(1)}, u32[]{:S(2)}, u32[]{:S(2)}) async-start(bf16[128,2,144]{2,1,0:T(2,128)(2,1)} %reshape.171), calls=%async_computation.2 | async-start | bytes 262144 | tf_op jit(solution)/shard_map/all_to_all | solution.py:32
  100.0 10.7 %all-to-all-done.2 = bf16[128,2,144]{2,1,0:T(2,128)(2,1)S(1)} async-done(((bf16[128,2,144]{2,1,0:T(2,128)(2,1)}), bf16[128,2,144]{2,1,0:T(2,128)(2,1)S(1)}, u32[]{:S(2)}, u32[]{:S(2)}) %all-to-all-start.2) | async-done | bytes 73760 | tf_op jit(solution)/shard_map/all_to_all | solution.py:32
  113.6 20.6 %all_gather.13 = bf16[4,96,384]{2,1,0:T(8,128)(2,1)S(1)} all-gather(bf16[1,96,384]{2,1,0:T(8,128)(2,1)S(1)} %all_gather_squeeze_reshape.3), channel_id=1, replica_groups=mesh['rq'=4,'rr'=8,'col'=16] {'rq'}, dimensions={0}, use_global_device_ids=true | all-gather | bytes 368640 | tf_op jit(solution)/shard_map/all_gather | solution.py:80
  135.6 1.4 all_to_all.44
  136.9 1.7 reduce.8
  138.7 0.9 reshape.173
  139.5 6.0 %all-to-all-start.3 = ((bf16[128,2,288]{2,1,0:T(2,128)(2,1)}), bf16[128,2,288]{2,1,0:T(2,128)(2,1)S(1)}, u32[]{:S(2)}, u32[]{:S(2)}) async-start(bf16[128,2,288]{2,1,0:T(2,128)(2,1)} %reshape.173), calls=%async_computation.3 | async-start | bytes 393216 | tf_op jit(solution)/shard_map/all_to_all | solution.py:32
  146.1 11.1 %all-to-all-done.3 = bf16[128,2,288]{2,1,0:T(2,128)(2,1)S(1)} async-done(((bf16[128,2,288]{2,1,0:T(2,128)(2,1)}), bf16[128,2,288]{2,1,0:T(2,128)(2,1)S(1)}, u32[]{:S(2)}, u32[]{:S(2)}) %all-to-all-start.3) | async-done | bytes 147488 | tf_op jit(solution)/shard_map/all_to_all | solution.py:32
  158.8 0.7 copy-done.4
  160.3 23.6 %all_to_all.53 = f32[128,8,128]{2,1,0:T(8,128)S(1)} all-to-all(f32[128,8,128]{2,1,0:T(8,128)S(1)} %bitcast.138), channel_id=1, replica_groups=mesh['rq'=4,'rr'=8,'col'=16] {'rr','col'}, dimensions={0} | all-to-all | bytes 1048576 | tf_op jit(solution)/shard_map/all_to_all | solution.py:32
  184.1 14.5 %all-gather = f32[32,128]{1,0:T(8,128)S(1)} all-gather(f32[8,128]{1,0:T(8,128)S(1)} %reduce_sum.129), channel_id=2, replica_groups=mesh['rq'=4,'rr'=8,'col'=16] {'rq'}, dimensions={0}, use_global_device_ids=true | all-gather | bytes 20480 | tf_op jit(solution)/shard_map/all_gather | solution.py:111
  198.6 0.8 broadcast_in_dim.8
  199.4 9.5 %all-to-all-start.5 = ((f32[128,8,128]{2,1,0:T(8,128)}), f32[128,8,128]{2,1,0:T(8,128)S(1)}, u32[]{:S(2)}, u32[]{:S(2)}) async-start(f32[128,8,128]{2,1,0:T(8,128)} %broadcast_in_dim.8), calls=%async_computation.5 | async-start | bytes 1048576 | tf_op jit(solution)/shard_map/all_to_all | solution.py:32
  208.9 0.9 multiply_convert_fusion
  209.8 17.4 %all-to-all-done.5 = f32[128,8,128]{2,1,0:T(8,128)S(1)} async-done(((f32[128,8,128]{2,1,0:T(8,128)}), f32[128,8,128]{2,1,0:T(8,128)S(1)}, u32[]{:S(2)}, u32[]{:S(2)}) %all-to-all-start.5) | async-done | bytes 524320 | tf_op jit(solution)/shard_map/all_to_all | solution.py:32
  227.7 0.6 slice_bitcast_fusion
  228.4 0.7 copy-done.5
  (85 shorter events, 13.3 us)
Async XLA Ops:
  0.6 89.4 %copy-start = (bf16[128,128]{1,0:T(8,128)(2,1)S(1)}, bf16[128,128]{1,0:T(8,128)(2,1)}, u32[]{:S(2)}) copy-start(bf16[128,128]{1,0:T(8,128)(2,1)} %param.15) | copy-start | bytes 98308
  0.6 1.1 copy-start.1
  1.9 0.7 copy-start.7
  1.9 0.7 copy-start.8
  2.0 1.4 copy-start.2
  89.2 0.7 copy-start.6
  89.2 0.7 copy-start.9
  90.0 0.9 copy-start.3
  90.0 1.0 copy-start.10
  94.0 16.7 %all-to-all-start.2 = ((bf16[128,2,144]{2,1,0:T(2,128)(2,1)}), bf16[128,2,144]{2,1,0:T(2,128)(2,1)S(1)}, u32[]{:S(2)}, u32[]{:S(2)}) async-start(bf16[128,2,144]{2,1,0:T(2,128)(2,1)} %reshape.171), calls=%async_computation.2 | async-start | bytes 262144 | tf_op jit(solution)/shard_map/all_to_all | solution.py:32
  139.5 17.7 %all-to-all-start.3 = ((bf16[128,2,288]{2,1,0:T(2,128)(2,1)}), bf16[128,2,288]{2,1,0:T(2,128)(2,1)S(1)}, u32[]{:S(2)}, u32[]{:S(2)}) async-start(bf16[128,2,288]{2,1,0:T(2,128)(2,1)} %reshape.173), calls=%async_computation.3 | async-start | bytes 393216 | tf_op jit(solution)/shard_map/all_to_all | solution.py:32
  158.5 0.9 copy-start.4
  199.4 27.7 %all-to-all-start.5 = ((f32[128,8,128]{2,1,0:T(8,128)}), f32[128,8,128]{2,1,0:T(8,128)S(1)}, u32[]{:S(2)}, u32[]{:S(2)}) async-start(f32[128,8,128]{2,1,0:T(8,128)} %broadcast_in_dim.8), calls=%async_computation.5 | async-start | bytes 1048576 | tf_op jit(solution)/shard_map/all_to_all | solution.py:32
  228.4 0.7 copy-start.5

commit v2 on v1

--- a/solution.py
+++ b/solution.py
@@ -3,7 +3,8 @@
 from jax import lax
 from jax.sharding import Mesh, PartitionSpec as P
 
-GROUP = ("rr", "col")
+GROUP = ("row", "xh", "yh")
+QUAD = ("xl", "core")
 BF = jnp.bfloat16
 F32 = jnp.float32
 
@@ -34,17 +35,24 @@
 
 def local(pair_in, cotangent, in_gain, in_bias, in_weights, out_gain, out_bias, out_weights):
     ni, nk, c = pair_in.shape
-    rr, cols, rq = lax.axis_size("rr"), lax.axis_size("col"), lax.axis_size("rq")
+    nrow, quads = lax.axis_size("row"), 4
     pairs = ni * nk
-    rows, all_k = rr * ni, cols * nk
+    rows, part = nrow * ni, quads * nk
+    quad = lax.axis_index(QUAD)
 
     def to_matrix(x):
-        x = x.reshape(rr, cols, -1, ni, nk).transpose(2, 0, 3, 1, 4)
-        return x.reshape(-1, rows, all_k)
+        return x.reshape(nrow, quads, ni, nk).transpose(0, 2, 1, 3).reshape(rows, part)
 
     def from_matrix(x):
-        x = x.reshape(-1, rr, ni, cols, nk).transpose(1, 3, 0, 2, 4)
-        return x.reshape(c, -1)
+        return x.reshape(nrow, ni, quads, nk).transpose(0, 2, 1, 3).reshape(c, pairs)
+
+    def to_blocks(x):
+        x = x.reshape(2, 2, 2, 2, nk // ni, quads, ni, nk).transpose(1, 3, 0, 2, 4, 6, 5, 7)
+        return x.reshape(quads, part, part)
+
+    def from_blocks(x):
+        x = x.reshape(2, 2, 2, 2, nk // ni, ni, quads, nk).transpose(2, 0, 3, 1, 4, 6, 5, 7)
+        return x.reshape(c, pairs)
 
     in_hat, in_rstd = stats(pair_in.reshape(pairs, c).astype(F32), 1)
     in_norm = (in_hat * in_gain + in_bias).astype(BF)
@@ -58,11 +66,13 @@
     right = (right_sig * lin_right).astype(BF)
 
     got = exchange(jnp.concatenate([left, right], axis=1))
-    mats = to_matrix(got)
-    gathered = lax.all_gather(mats, "rq")
-    left_all = gathered[:, 0].reshape(rq * rows, all_k)
-    right_all = gathered[:, 1].reshape(rq * rows, all_k)
-    product = dot(mats[0], right_all, 1, 1)
+    left_own = to_matrix(got[:, :pairs])
+    right_own = to_blocks(got[:, pairs:])
+    gathered = lax.all_gather(jnp.stack([left_own, right_own.reshape(rows, part)]), QUAD)
+    product = jnp.zeros((rows, part), F32)
+    for q in range(quads):
+        picked = lax.dynamic_slice_in_dim(gathered[q, 1], quad * part, part, 0)
+        product = product + dot(gathered[q, 0], picked, 1, 1)
     prod = exchange(from_matrix(product))
 
     out_hat, out_rstd = stats(prod, 0)
@@ -76,12 +86,15 @@
     d_outnorm = dot(out_weights, d_lin, 1, 1)
     d_product = back(d_outnorm, out_hat, out_rstd, gain_col, 0).astype(BF)
 
-    d_mat = to_matrix(exchange(d_product))[0]
-    d_all = lax.all_gather(d_mat, "rq").reshape(rq * rows, all_k)
-    d_left_m = dot(d_mat, right_all, 1, 0).astype(BF)
-    d_right_m = dot(d_all, left_all, 0, 0).astype(BF)
-    d_right_m = lax.dynamic_slice_in_dim(d_right_m, lax.axis_index("rq") * rows, rows, 0)
-    d_both = exchange(from_matrix(jnp.stack([d_left_m, d_right_m]))).astype(F32)
+    d_all = lax.all_gather(to_matrix(exchange(d_product)), QUAD)
+    d_left_m = jnp.zeros((rows, part), F32)
+    d_right_m = []
+    for q in range(quads):
+        d_left_m = d_left_m + dot(d_all[q], right_own[q], 1, 0)
+        d_right_m.append(dot(d_all[q], left_own, 0, 0).astype(BF))
+    d_left_s = from_matrix(d_left_m.astype(BF))
+    d_right_s = from_blocks(jnp.concatenate(d_right_m))
+    d_both = exchange(jnp.concatenate([d_left_s, d_right_s], axis=1)).astype(F32)
     d_left, d_right = d_both[:, :pairs], d_both[:, pairs:]
 
     d_proj = [
@@ -102,16 +115,17 @@
             jnp.sum(d_outnorm, axis=1),
         ]
     )
-    blocks = [dot(in_norm, part, 0, 1) for part in d_proj]
+    blocks = [dot(in_norm, d, 0, 1) for d in d_proj]
     blocks += [dot(in_norm, d_five, 0, 0), dot(out_norm, d_lin, 1, 0), norms]
-    used = 6 * c + 4
-    slots = 8 * c
-    stacked = jnp.concatenate(blocks + [jnp.zeros((slots - used, c), F32)])
-    mine = jnp.sum(exchange(stacked.reshape(c, 8, c)), axis=0)
-    quarter = lax.all_gather(mine, "rq")
-    total = (quarter[0] + quarter[1]) + (quarter[2] + quarter[3])
-    total = total * (1.0 / all_k)
-    summed = exchange(jnp.broadcast_to(total[None], (c, 8, c))).reshape(slots, c)
+    used, share, slots = 6 * c + 4, 200, 2
+    stacked = jnp.concatenate(blocks + [jnp.zeros((quads * share - used, c), F32)])
+    ours = lax.all_to_all(
+        stacked.reshape(quads, share, c), QUAD, split_axis=0, concat_axis=0, tiled=True
+    )
+    ours = jnp.pad(jnp.sum(ours, axis=0), ((0, slots * c - share), (0, 0)))
+    mine = jnp.sum(exchange(ours.reshape(c, slots, c)), axis=0) * (1.0 / rows)
+    summed = exchange(jnp.broadcast_to(mine[None], (c, slots, c))).reshape(slots * c, c)
+    summed = lax.all_gather(summed[:share], QUAD).reshape(quads * share, c)
     grad_in = jnp.concatenate([summed[b * c : (b + 1) * c] for b in range(5)], axis=1)
     return (
         pair_out.reshape(ni, nk, c),
@@ -123,9 +137,9 @@
 
 
 def solution(mesh):
-    grid = mesh.devices.reshape(4, mesh.devices.shape[0] // 4, mesh.devices.shape[1])
-    split = Mesh(grid, ("rq", "rr", "col"))
-    pair = P(("rq", "rr"), "col", None)
+    grid = mesh.devices.reshape(mesh.devices.shape[0], 2, 2, 2, 2)
+    split = Mesh(grid, ("row", "xh", "xl", "yh", "core"))
+    pair = P("row", ("xh", "xl", "yh", "core"), None)
     return jax.shard_map(
         local,
         mesh=split,

time: 230 us -> 234 us (1.017)
  blocking collectives: 136 us -> 90.6 us
  starting transfers between devices: 21.4 us -> 48.3 us
  waiting for transfers between devices: 39.2 us -> 62.8 us
    all_gather x3, blocking collectives: 69.6 us -> 29.6 us  [the longest x1 11.2 us: local(): lax.all_gather(jnp.stack([left_own, right_own.reshape(rows, part)]), QUAD)]
    all_to_all x3 -> x4, starting transfers between devices: 21.4 us -> 48.3 us  [exchange(): return lax.all_to_all(x, GROUP, split_axis=0, concat_axis=0, tiled=True)]
    all_to_all x3 -> x4, waiting for transfers between devices: 39.2 us -> 62.8 us  [exchange(): return lax.all_to_all(x, GROUP, split_axis=0, concat_axis=0, tiled=True)]
    all_to_all x3 -> x2, blocking collectives: 66.7 us -> 48 us  [exchange(): return lax.all_to_all(x, GROUP, split_axis=0, concat_axis=0, tiled=True)]
    all_to_all x0 -> x1, blocking collectives: none -> 13 us  [local(): lax.all_to_all(stacked.reshape(quads, share, c), QUAD, split_axis=0, conc...]
    dot_general x15 -> x24, matrix products: 4.47 us -> 6.32 us  [dot(): lax.dot_general(a, b, (((da,), (db,)), ((), ())), preferred_element_type=...]
    unnamed x34 -> x42, local copies, waits for them, and re-layouts: 6.22 us -> 6.71 us
  transfers between devices with their start and end apart: 3 -> 4, of which waited for: 3 -> 4; matrix products, arithmetic and copies ran while one was open for 1% -> 1% of each run, Pallas kernels for 0% -> 0%
where the time goes in v2:
time: 234 us; the launch traced here: 233 us
  blocking collectives  90.6 us (39%)
  waiting for transfers between devices  62.8 us (27%)
  starting transfers between devices  48.3 us (21%)
  local copies, waits for them, and re-layouts  16.8 us (7%)
  other arithmetic  7.07 us (3%)
  matrix products  6.32 us (3%)
    all_to_all x4, waiting for transfers between devices, exchange(): return lax.all_to_all(x, GROUP, split_axis=0, concat_axis=0, tiled=True)  62.8 us
    all_to_all x4, starting transfers between devices, exchange(): return lax.all_to_all(x, GROUP, split_axis=0, concat_axis=0, tiled=True)  48.3 us
    all_to_all x2, blocking collectives, exchange(): return lax.all_to_all(x, GROUP, split_axis=0, concat_axis=0, tiled=True)  48 us
    all_to_all x1, blocking collectives, local(): lax.all_to_all(stacked.reshape(quads, share, c), QUAD, split_axis=0, conc...  13 us
    all_gather x1, blocking collectives, local(): lax.all_gather(jnp.stack([left_own, right_own.reshape(rows, part)]), QUAD)  11.2 us
    all_gather x1, blocking collectives, local(): summed = lax.all_gather(summed[:share], QUAD).reshape(quads * share, c)  9.43 us
    all_gather x1, blocking collectives, local(): d_all = lax.all_gather(to_matrix(exchange(d_product)), QUAD)  8.97 us
    unnamed x42, local copies, waits for them, and re-layouts  6.71 us
  transfers between devices with their start and end apart: 4, of which 4 were waited for; matrix products, arithmetic and copies ran while one was open for 1% of the time, Pallas kernels for 0%

profile of v2, /device:TPU:1, one launch (start us, length us, event | category | flops | bytes accessed | tf_op | source)
XLA Modules:
  0.0 233.1 jit_solution(3225542326249699988)
XLA Ops:
  0.7 1.1 convert_reduce_fusion
  2.5 0.8 fusion.22
  4.2 0.7 reduce.5
  5.0 0.9 reshape.168
  5.9 23.0 %all-to-all-start = ((bf16[128,2,288]{2,1,0:T(2,128)(2,1)}), bf16[128,2,288]{2,1,0:T(2,128)(2,1)S(1)}, u32[]{:S(2)}, u32[]{:S(2)}) async-start(bf16[128,2,288]{2,1,0:T(2,128)(2,1)} %reshape.168), calls=%async_computation | async-start | bytes 393216 | tf_op jit(solution)/shard_map/all_to_all | solution.py:33
  28.9 16.4 %all-to-all-done = bf16[128,2,288]{2,1,0:T(2,128)(2,1)S(1)} async-done(((bf16[128,2,288]{2,1,0:T(2,128)(2,1)}), bf16[128,2,288]{2,1,0:T(2,128)(2,1)S(1)}, u32[]{:S(2)}, u32[]{:S(2)}) %all-to-all-start) | async-done | bytes 147488 | tf_op jit(solution)/shard_map/all_to_all | solution.py:33
  48.2 11.2 %all-gather = bf16[8,384,96]{1,2,0:T(8,128)(2,1)S(1)} all-gather(bf16[2,384,96]{1,2,0:T(8,128)(2,1)S(1)} %copy.102), channel_id=2, replica_groups=mesh['row'=32,'xh'=2,'xl'=2,'yh'=2,'core'=2] {'xl','core'}, dimensions={0}, use_global_device_ids=true | all-gather | bytes 737280 | tf_op jit(solution)/shard_map/all_gather | solution.py:71
  61.2 0.6 all_to_all.50
  61.8 24.5 %all_to_all.58 = f32[128,1,288]{2,1,0:T(1,128)S(1)} all-to-all(f32[128,1,288]{2,1,0:T(1,128)S(1)} %all_to_all.50), channel_id=1, replica_groups=mesh['row'=32,'xh'=2,'xl'=2,'yh'=2,'core'=2] {'row','xh','yh'}, dimensions={0} | all-to-all | bytes 294912 | tf_op jit(solution)/shard_map/all_to_all | solution.py:33
  86.9 0.6 copy-done.9
  87.9 0.7 copy-done.14
  88.6 0.9 fusion.14
  90.0 0.7 reduce.6
  90.8 0.8 reshape.170
  91.6 10.4 %all-to-all-start.2 = ((bf16[128,2,144]{2,1,0:T(2,128)(2,1)}), bf16[128,2,144]{2,1,0:T(2,128)(2,1)S(1)}, u32[]{:S(2)}, u32[]{:S(2)}) async-start(bf16[128,2,144]{2,1,0:T(2,128)(2,1)} %reshape.170), calls=%async_computation.2 | async-start | bytes 262144 | tf_op jit(solution)/shard_map/all_to_all | solution.py:33
  102.5 15.1 %all-to-all-done.2 = bf16[128,2,144]{2,1,0:T(2,128)(2,1)S(1)} async-done(((bf16[128,2,144]{2,1,0:T(2,128)(2,1)}), bf16[128,2,144]{2,1,0:T(2,128)(2,1)S(1)}, u32[]{:S(2)}, u32[]{:S(2)}) %all-to-all-start.2) | async-done | bytes 73760 | tf_op jit(solution)/shard_map/all_to_all | solution.py:33
  117.8 0.6 reduce.4
  119.5 9.0 %all_gather.17 = bf16[4,384,96]{1,2,0:T(8,128)(2,1)S(1)} all-gather(bf16[1,384,96]{1,2,0:T(8,128)(2,1)S(1)} %copy.109), channel_id=1, replica_groups=mesh['row'=32,'xh'=2,'xl'=2,'yh'=2,'core'=2] {'xl','core'}, dimensions={0}, use_global_device_ids=true | all-gather | bytes 368640 | tf_op jit(solution)/shard_map/all_gather | solution.py:89
  132.2 0.7 reduce.7
  132.9 0.9 reshape.172
  133.7 6.4 %all-to-all-start.3 = ((bf16[128,2,288]{2,1,0:T(2,128)(2,1)}), bf16[128,2,288]{2,1,0:T(2,128)(2,1)S(1)}, u32[]{:S(2)}, u32[]{:S(2)}) async-start(bf16[128,2,288]{2,1,0:T(2,128)(2,1)} %reshape.172), calls=%async_computation.3 | async-start | bytes 393216 | tf_op jit(solution)/shard_map/all_to_all | solution.py:33
  140.7 16.3 %all-to-all-done.3 = bf16[128,2,288]{2,1,0:T(2,128)(2,1)S(1)} async-done(((bf16[128,2,288]{2,1,0:T(2,128)(2,1)}), bf16[128,2,288]{2,1,0:T(2,128)(2,1)S(1)}, u32[]{:S(2)}, u32[]{:S(2)}) %all-to-all-start.3) | async-done | bytes 147488 | tf_op jit(solution)/shard_map/all_to_all | solution.py:33
  158.6 0.6 copy-done.3
  159.9 13.0 %all_to_all.59 = f32[4,200,128]{2,1,0:T(8,128)S(1)} all-to-all(f32[4,200,128]{2,1,0:T(8,128)S(1)} %bitcast.156), channel_id=1, replica_groups=mesh['row'=32,'xh'=2,'xl'=2,'yh'=2,'core'=2] {'xl','core'}, dimensions={0} | all-to-all | bytes 819200 | tf_op jit(solution)/shard_map/all_to_all | solution.py:122
  172.9 23.5 %all_to_all.60 = f32[128,2,128]{2,1,0:T(2,128)S(1)} all-to-all(f32[128,2,128]{2,1,0:T(2,128)S(1)} %bitcast.166), channel_id=1, replica_groups=mesh['row'=32,'xh'=2,'xl'=2,'yh'=2,'core'=2] {'row','xh','yh'}, dimensions={0} | all-to-all | bytes 262144 | tf_op jit(solution)/shard_map/all_to_all | solution.py:33
  196.6 0.7 broadcast_in_dim.5
  197.3 8.6 %all-to-all-start.6 = ((f32[128,2,128]{2,1,0:T(2,128)}), f32[128,2,128]{2,1,0:T(2,128)S(1)}, u32[]{:S(2)}, u32[]{:S(2)}) async-start(f32[128,2,128]{2,1,0:T(2,128)} %broadcast_in_dim.5), calls=%async_computation.6 | async-start | bytes 262144 | tf_op jit(solution)/shard_map/all_to_all | solution.py:33
  205.9 0.9 multiply_convert_fusion
  206.8 14.9 %all-to-all-done.6 = f32[128,2,128]{2,1,0:T(2,128)S(1)} async-done(((f32[128,2,128]{2,1,0:T(2,128)}), f32[128,2,128]{2,1,0:T(2,128)S(1)}, u32[]{:S(2)}, u32[]{:S(2)}) %all-to-all-start.6) | async-done | bytes 131104 | tf_op jit(solution)/shard_map/all_to_all | solution.py:33
  221.7 9.4 %all_gather.19 = f32[4,200,128]{2,1,0:T(8,128)S(1)} all-gather(f32[1,200,128]{2,1,0:T(8,128)S(1)} %bitcast.167), channel_id=1, replica_groups=mesh['row'=32,'xh'=2,'xl'=2,'yh'=2,'core'=2] {'xl','core'}, dimensions={0}, use_global_device_ids=true | all-gather | bytes 512000 | tf_op jit(solution)/shard_map/all_gather | solution.py:128
  231.8 0.6 fusion.48
  232.4 0.7 copy-done.8
  (120 shorter events, 16.8 us)
Async XLA Ops:
  0.6 87.1 %copy-start = (bf16[128,128]{1,0:T(8,128)(2,1)S(1)}, bf16[128,128]{1,0:T(8,128)(2,1)}, u32[]{:S(2)}) copy-start(bf16[128,128]{1,0:T(8,128)(2,1)} %param.15) | copy-start | bytes 98308
  0.6 1.2 copy-start.1
  1.8 0.6 copy-start.4
  1.8 0.7 copy-start.10
  1.8 0.7 copy-start.12
  2.1 1.3 copy-start.2
  2.5 0.8 copy-start.6
  5.9 39.4 %all-to-all-start = ((bf16[128,2,288]{2,1,0:T(2,128)(2,1)}), bf16[128,2,288]{2,1,0:T(2,128)(2,1)S(1)}, u32[]{:S(2)}, u32[]{:S(2)}) async-start(bf16[128,2,288]{2,1,0:T(2,128)(2,1)} %reshape.168), calls=%async_computation | async-start | bytes 393216 | tf_op jit(solution)/shard_map/all_to_all | solution.py:33
  86.9 0.7 copy-start.9
  86.9 0.7 copy-start.13
  87.7 0.9 copy-start.14
  91.6 26.0 %all-to-all-start.2 = ((bf16[128,2,144]{2,1,0:T(2,128)(2,1)}), bf16[128,2,144]{2,1,0:T(2,128)(2,1)S(1)}, u32[]{:S(2)}, u32[]{:S(2)}) async-start(bf16[128,2,144]{2,1,0:T(2,128)(2,1)} %reshape.170), calls=%async_computation.2 | async-start | bytes 262144 | tf_op jit(solution)/shard_map/all_to_all | solution.py:33
  133.7 23.3 %all-to-all-start.3 = ((bf16[128,2,288]{2,1,0:T(2,128)(2,1)}), bf16[128,2,288]{2,1,0:T(2,128)(2,1)S(1)}, u32[]{:S(2)}, u32[]{:S(2)}) async-start(bf16[128,2,288]{2,1,0:T(2,128)(2,1)} %reshape.172), calls=%async_computation.3 | async-start | bytes 393216 | tf_op jit(solution)/shard_map/all_to_all | solution.py:33
  158.3 0.9 copy-start.3
  158.4 0.9 copy-start.5
  158.4 0.9 copy-start.7
  158.6 0.7 copy-start.11
  197.3 24.4 %all-to-all-start.6 = ((f32[128,2,128]{2,1,0:T(2,128)}), f32[128,2,128]{2,1,0:T(2,128)S(1)}, u32[]{:S(2)}, u32[]{:S(2)}) async-start(f32[128,2,128]{2,1,0:T(2,128)} %broadcast_in_dim.5), calls=%async_computation.6 | async-start | bytes 262144 | tf_op jit(solution)/shard_map/all_to_all | solution.py:33
  232.4 0.7 copy-start.8

commit v3 on v1

--- a/solution.py
+++ b/solution.py
@@ -3,7 +3,9 @@
 from jax import lax
 from jax.sharding import Mesh, PartitionSpec as P
 
-GROUP = ("rr", "col")
+CUBE = ("zr", "yl", "xh", "xl", "yh", "core")
+MID = ("zr", "yl", "xh", "yh")
+QUAD = ("xl", "core")
 BF = jnp.bfloat16
 F32 = jnp.float32
 
@@ -28,23 +30,23 @@
     )
 
 
-def exchange(x):
-    return lax.all_to_all(x, GROUP, split_axis=0, concat_axis=0, tiled=True)
+def exchange(x, axes=CUBE):
+    return lax.all_to_all(x, axes, split_axis=0, concat_axis=0, tiled=True)
 
 
 def local(pair_in, cotangent, in_gain, in_bias, in_weights, out_gain, out_bias, out_weights):
     ni, nk, c = pair_in.shape
-    rr, cols, rq = lax.axis_size("rr"), lax.axis_size("col"), lax.axis_size("rq")
+    rr, cols, quarters = 8, 16, 4
     pairs = ni * nk
     rows, all_k = rr * ni, cols * nk
 
     def to_matrix(x):
-        x = x.reshape(rr, cols, -1, ni, nk).transpose(2, 0, 3, 1, 4)
-        return x.reshape(-1, rows, all_k)
+        x = x.reshape(rr, cols, ni, nk).transpose(0, 2, 1, 3)
+        return x.reshape(rows, all_k)
 
     def from_matrix(x):
-        x = x.reshape(-1, rr, ni, cols, nk).transpose(1, 3, 0, 2, 4)
-        return x.reshape(c, -1)
+        x = x.reshape(rr, ni, cols, nk).transpose(0, 2, 1, 3)
+        return x.reshape(c, pairs)
 
     in_hat, in_rstd = stats(pair_in.reshape(pairs, c).astype(F32), 1)
     in_norm = (in_hat * in_gain + in_bias).astype(BF)
@@ -58,11 +60,9 @@
     right = (right_sig * lin_right).astype(BF)
 
     got = exchange(jnp.concatenate([left, right], axis=1))
-    mats = to_matrix(got)
-    gathered = lax.all_gather(mats, "rq")
-    left_all = gathered[:, 0].reshape(rq * rows, all_k)
-    right_all = gathered[:, 1].reshape(rq * rows, all_k)
-    product = dot(mats[0], right_all, 1, 1)
+    left_own = to_matrix(got[:, :pairs])
+    right_all = lax.all_gather(to_matrix(got[:, pairs:]), "zq").reshape(all_k, all_k)
+    product = dot(left_own, right_all, 1, 1)
     prod = exchange(from_matrix(product))
 
     out_hat, out_rstd = stats(prod, 0)
@@ -76,12 +76,13 @@
     d_outnorm = dot(out_weights, d_lin, 1, 1)
     d_product = back(d_outnorm, out_hat, out_rstd, gain_col, 0).astype(BF)
 
-    d_mat = to_matrix(exchange(d_product))[0]
-    d_all = lax.all_gather(d_mat, "rq").reshape(rq * rows, all_k)
+    d_mat = to_matrix(exchange(d_product))
     d_left_m = dot(d_mat, right_all, 1, 0).astype(BF)
-    d_right_m = dot(d_all, left_all, 0, 0).astype(BF)
-    d_right_m = lax.dynamic_slice_in_dim(d_right_m, lax.axis_index("rq") * rows, rows, 0)
-    d_both = exchange(from_matrix(jnp.stack([d_left_m, d_right_m]))).astype(F32)
+    terms = dot(d_mat, left_own, 0, 0).astype(BF)
+    terms = exchange(terms.reshape(quarters, rows, all_k), ("zq",))
+    d_right_m = jnp.sum(terms.astype(F32), axis=0).astype(BF)
+    d_both = exchange(jnp.concatenate([from_matrix(d_left_m), from_matrix(d_right_m)], axis=1))
+    d_both = d_both.astype(F32)
     d_left, d_right = d_both[:, :pairs], d_both[:, pairs:]
 
     d_proj = [
@@ -104,14 +105,16 @@
     )
     blocks = [dot(in_norm, part, 0, 1) for part in d_proj]
     blocks += [dot(in_norm, d_five, 0, 0), dot(out_norm, d_lin, 1, 0), norms]
-    used = 6 * c + 4
-    slots = 8 * c
-    stacked = jnp.concatenate(blocks + [jnp.zeros((slots - used, c), F32)])
-    mine = jnp.sum(exchange(stacked.reshape(c, 8, c)), axis=0)
-    quarter = lax.all_gather(mine, "rq")
-    total = (quarter[0] + quarter[1]) + (quarter[2] + quarter[3])
-    total = total * (1.0 / all_k)
-    summed = exchange(jnp.broadcast_to(total[None], (c, 8, c))).reshape(slots, c)
+    used, share, slots = 6 * c + 4, 200, 256
+    stacked = jnp.concatenate(blocks + [jnp.zeros((4 * share - used, c), F32)])
+    ours = jnp.sum(exchange(stacked.reshape(4, share, c), QUAD), axis=0)
+    ours = jnp.pad(ours, ((0, slots - share), (0, 0))).reshape(32, slots // 32, c)
+    mine = jnp.sum(exchange(ours, MID), axis=0)
+    mine = mine + lax.ppermute(mine, "zq", [(0, 3), (3, 0), (1, 2), (2, 1)])
+    mine = mine + lax.ppermute(mine, "zq", [(0, 1), (1, 0), (2, 3), (3, 2)])
+    mine = jnp.broadcast_to((mine * (1.0 / all_k))[None], ours.shape)
+    summed = exchange(mine, MID).reshape(slots, c)
+    summed = lax.all_gather(summed[:share], QUAD).reshape(4 * share, c)
     grad_in = jnp.concatenate([summed[b * c : (b + 1) * c] for b in range(5)], axis=1)
     return (
         pair_out.reshape(ni, nk, c),
@@ -123,9 +126,9 @@
 
 
 def solution(mesh):
-    grid = mesh.devices.reshape(4, mesh.devices.shape[0] // 4, mesh.devices.shape[1])
-    split = Mesh(grid, ("rq", "rr", "col"))
-    pair = P(("rq", "rr"), "col", None)
+    grid = mesh.devices.reshape(4, 4, 2, 2, 2, 2, 2)
+    split = Mesh(grid, ("zq", "zr", "yl", "xh", "xl", "yh", "core"))
+    pair = P(("zq", "zr", "yl"), ("xh", "xl", "yh", "core"), None)
     return jax.shard_map(
         local,
         mesh=split,

time: 230 us -> 221 us (0.961)
  blocking collectives: 136 us -> 104 us
  waiting for transfers between devices: 39.2 us -> 55.1 us
  starting transfers between devices: 21.4 us -> 34 us
  other arithmetic: 9.01 us -> 6.2 us
    all_gather x3 -> x2, blocking collectives: 69.6 us -> 36.2 us  [the longest x1 24.9 us: local(): lax.all_gather(to_matrix(got[:, pairs:]), 'zq').reshape(all_k, all_k)]
    ppermute x0 -> x2, waiting for transfers between devices: none -> 8.72 us  [the longest x1 4.55 us: local(): mine = mine + lax.ppermute(mine, 'zq', [(0, 1), (1, 0), (2, 3), (3, 2)])]
    ppermute x0 -> x2, starting transfers between devices: none -> 7.77 us  [the longest x1 4.08 us: local(): mine = mine + lax.ppermute(mine, 'zq', [(0, 3), (3, 0), (1, 2), (2, 1)])]
    all_to_all x3 -> x4, waiting for transfers between devices: 39.2 us -> 46.4 us  [exchange(): return lax.all_to_all(x, axes, split_axis=0, concat_axis=0, tiled=True)]
    all_to_all x3 -> x4, starting transfers between devices: 21.4 us -> 26.2 us  [exchange(): return lax.all_to_all(x, axes, split_axis=0, concat_axis=0, tiled=True)]
    another operation x7 -> x1, local copies, waits for them, and re-layouts: 3.07 us -> 0.37 us  [local(): lax.all_gather(to_matrix(got[:, pairs:]), 'zq').reshape(all_k, all_k)]
    all_to_all x3 -> x4, blocking collectives: 66.7 us -> 67.4 us  [exchange(): return lax.all_to_all(x, axes, split_axis=0, concat_axis=0, tiled=True)]
    unnamed x34 -> x30, local copies, waits for them, and re-layouts: 6.22 us -> 5.66 us
  transfers between devices with their start and end apart: 3 -> 6, of which waited for: 3 -> 6; matrix products, arithmetic and copies ran while one was open for 1% -> 1% of each run, Pallas kernels for 0% -> 0%
where the time goes in v3:
time: 221 us
  blocking collectives  104 us (47%)
  waiting for transfers between devices  55.1 us (25%)
  starting transfers between devices  34 us (15%)
  local copies, waits for them, and re-layouts  15.5 us (7%)
  other arithmetic  6.2 us (3%)
  matrix products  5.08 us (2%)
    all_to_all x4, blocking collectives, exchange(): return lax.all_to_all(x, axes, split_axis=0, concat_axis=0, tiled=True)  67.4 us
    all_to_all x4, waiting for transfers between devices, exchange(): return lax.all_to_all(x, axes, split_axis=0, concat_axis=0, tiled=True)  46.4 us
    all_to_all x4, starting transfers between devices, exchange(): return lax.all_to_all(x, axes, split_axis=0, concat_axis=0, tiled=True)  26.2 us
    all_gather x1, blocking collectives, local(): lax.all_gather(to_matrix(got[:, pairs:]), 'zq').reshape(all_k, all_k)  24.9 us
    all_gather x1, blocking collectives, local(): summed = lax.all_gather(summed[:share], QUAD).reshape(4 * share, c)  11.4 us
    unnamed x30, local copies, waits for them, and re-layouts  5.66 us
    dot_general x15, matrix products, dot(): lax.dot_general(a, b, (((da,), (db,)), ((), ())), preferred_element_type=...  5.08 us
    ppermute x1, waiting for transfers between devices, local(): mine = mine + lax.ppermute(mine, 'zq', [(0, 1), (1, 0), (2, 3), (3, 2)])  4.55 us
  transfers between devices with their start and end apart: 6, of which 6 were waited for; matrix products, arithmetic and copies ran while one was open for 1% of the time, Pallas kernels for 0%

profile of v3, /device:TPU:1, one launch (start us, length us, event | category | flops | bytes accessed | tf_op | source)
XLA Modules:
  0.0 220.7 jit_solution(5808394492121867365)
XLA Ops:
  0.7 1.1 convert_reduce_fusion
  3.8 0.7 reduce.6
  4.9 25.4 %all_to_all.63 = bf16[128,2,288]{2,1,0:T(2,128)(2,1)S(1)} all-to-all(bf16[128,2,288]{2,1,0:T(2,128)(2,1)S(1)} %reshape.174), channel_id=1, replica_groups=mesh['zq'=4,'zr'=4,'yl'=2,'xh'=2,'xl'=2,'yh'=2,'core'=2] {'zr','yl','xh'..., dimensions={0} | all-to-all | bytes 294912 | tf_op jit(solution)/shard_map/all_to_all | solution.py:34
  32.1 24.9 %all_gather.9 = bf16[4,96,384]{2,1,0:T(8,128)(2,1)S(1)} all-gather(bf16[1,96,384]{2,1,0:T(8,128)(2,1)S(1)} %all_gather_reshape.3), channel_id=1, replica_groups=mesh['zq'=4,'zr'=4,'yl'=2,'xh'=2,'xl'=2,'yh'=2,'core'=2] {'zq'}, dimensions={0}, use_global_device_ids=true | all-gather | bytes 368640 | tf_op jit(solution)/shard_map/all_gather | solution.py:64
  58.5 0.6 all_to_all.54
  59.2 18.7 %all_to_all.64 = f32[128,1,288]{2,1,0:T(1,128)S(1)} all-to-all(f32[128,1,288]{2,1,0:T(1,128)S(1)} %all_to_all.54), channel_id=1, replica_groups=mesh['zq'=4,'zr'=4,'yl'=2,'xh'=2,'xl'=2,'yh'=2,'core'=2] {'zr','yl','xh'..., dimensions={0} | all-to-all | bytes 294912 | tf_op jit(solution)/shard_map/all_to_all | solution.py:34
  79.4 0.7 copy-done.8
  80.1 0.9 fusion.13
  81.6 0.7 reduce.7
  82.4 0.8 reshape.176
  83.1 5.8 %all-to-all-start.2 = ((bf16[128,2,144]{2,1,0:T(2,128)(2,1)}), bf16[128,2,144]{2,1,0:T(2,128)(2,1)S(1)}, u32[]{:S(2)}, u32[]{:S(2)}) async-start(bf16[128,2,144]{2,1,0:T(2,128)(2,1)} %reshape.176), calls=%async_computation.2 | async-start | bytes 262144 | tf_op jit(solution)/shard_map/all_to_all | solution.py:34
  89.3 10.4 %all-to-all-done.2 = bf16[128,2,144]{2,1,0:T(2,128)(2,1)S(1)} async-done(((bf16[128,2,144]{2,1,0:T(2,128)(2,1)}), bf16[128,2,144]{2,1,0:T(2,128)(2,1)S(1)}, u32[]{:S(2)}, u32[]{:S(2)}) %all-to-all-start.2) | async-done | bytes 73760 | tf_op jit(solution)/shard_map/all_to_all | solution.py:34
  101.5 1.0 convolution_convert_fusion
  102.5 6.4 %all-to-all-start.3 = ((bf16[4,96,384]{2,1,0:T(8,128)(2,1)}), bf16[4,96,384]{2,1,0:T(8,128)(2,1)S(1)}, u32[]{:S(2)}, u32[]{:S(2)}) async-start(bf16[4,96,384]{2,1,0:T(8,128)(2,1)} %bitcast.18), calls=%async_computation.3 | async-start | bytes 589824 | tf_op jit(solution)/shard_map/all_to_all | solution.py:34
  110.1 16.1 %all-to-all-done.3 = bf16[4,96,384]{2,1,0:T(8,128)(2,1)S(1)} async-done(((bf16[4,96,384]{2,1,0:T(8,128)(2,1)}), bf16[4,96,384]{2,1,0:T(8,128)(2,1)S(1)}, u32[]{:S(2)}, u32[]{:S(2)}) %all-to-all-start.3) | async-done | bytes 294944 | tf_op jit(solution)/shard_map/all_to_all | solution.py:34
  127.4 0.7 reduce.8
  128.1 0.9 reshape.178
  129.0 10.2 %all-to-all-start.4 = ((bf16[128,2,288]{2,1,0:T(2,128)(2,1)}), bf16[128,2,288]{2,1,0:T(2,128)(2,1)S(1)}, u32[]{:S(2)}, u32[]{:S(2)}) async-start(bf16[128,2,288]{2,1,0:T(2,128)(2,1)} %reshape.178), calls=%async_computation.4 | async-start | bytes 393216 | tf_op jit(solution)/shard_map/all_to_all | solution.py:34
  139.8 11.1 %all-to-all-done.4 = bf16[128,2,288]{2,1,0:T(2,128)(2,1)S(1)} async-done(((bf16[128,2,288]{2,1,0:T(2,128)(2,1)}), bf16[128,2,288]{2,1,0:T(2,128)(2,1)S(1)}, u32[]{:S(2)}, u32[]{:S(2)}) %all-to-all-start.4) | async-done | bytes 147488 | tf_op jit(solution)/shard_map/all_to_all | solution.py:34
  153.1 10.1 %all_to_all.65 = f32[4,200,128]{2,1,0:T(8,128)S(1)} all-to-all(f32[4,200,128]{2,1,0:T(8,128)S(1)} %bitcast.122), channel_id=1, replica_groups=mesh['zq'=4,'zr'=4,'yl'=2,'xh'=2,'xl'=2,'yh'=2,'core'=2] {'xl','core'}, dimensions={0} | all-to-all | bytes 819200 | tf_op jit(solution)/shard_map/all_to_all | solution.py:34
  163.2 13.3 %all_to_all.66 = f32[32,8,128]{2,1,0:T(8,128)S(1)} all-to-all(f32[32,8,128]{2,1,0:T(8,128)S(1)} %pad_bitcast_fusion), channel_id=1, replica_groups=mesh['zq'=4,'zr'=4,'yl'=2,'xh'=2,'xl'=2,'yh'=2,'core'=2] {'zr','yl','xh'..., dimensions={0} | all-to-all | bytes 262144 | tf_op jit(solution)/shard_map/all_to_all | solution.py:34
  176.5 4.1 %collective-permute-start = (f32[8,128]{1,0:T(8,128)S(1)}, f32[8,128]{1,0:T(8,128)S(1)}, u32[]{:S(2)}, u32[]{:S(2)}) collective-permute-start(f32[8,128]{1,0:T(8,128)S(1)} %reduce_sum.152), channel_id=1, source_target_pairs={{0,384},{384,0},{128,256},{256,128},{1,385},{385,1},{129,257},{257... | collective-permute-start | bytes 12296 | tf_op jit(solution)/shard_map/ppermute | solution.py:113
  180.6 4.2 %collective-permute-done = f32[8,128]{1,0:T(8,128)S(1)} collective-permute-done((f32[8,128]{1,0:T(8,128)S(1)}, f32[8,128]{1,0:T(8,128)S(1)}, u32[]{:S(2)}, u32[]{:S(2)}) %collective-permute-start) | collective-permute-done | bytes 4128 | tf_op jit(solution)/shard_map/ppermute | solution.py:113
  184.8 3.7 %collective-permute-start.1 = (f32[8,128]{1,0:T(8,128)S(1)}, f32[8,128]{1,0:T(8,128)S(1)}, u32[]{:S(2)}, u32[]{:S(2)}) collective-permute-start(f32[8,128]{1,0:T(8,128)S(1)} %add.71), channel_id=1, source_target_pairs={{0,128},{128,0},{256,384},{384,256},{1,129},{129,1},{257,385},{385... | collective-permute-start | bytes 12296 | tf_op jit(solution)/shard_map/ppermute | solution.py:114
  188.5 4.5 %collective-permute-done.1 = f32[8,128]{1,0:T(8,128)S(1)} collective-permute-done((f32[8,128]{1,0:T(8,128)S(1)}, f32[8,128]{1,0:T(8,128)S(1)}, u32[]{:S(2)}, u32[]{:S(2)}) %collective-permute-start.1) | collective-permute-done | bytes 4128 | tf_op jit(solution)/shard_map/ppermute | solution.py:114
  193.0 0.7 broadcast_in_dim.5
  193.7 3.9 %all-to-all-start.7 = ((f32[32,8,128]{2,1,0:T(8,128)}), f32[32,8,128]{2,1,0:T(8,128)S(1)}, u32[]{:S(2)}, u32[]{:S(2)}) async-start(f32[32,8,128]{2,1,0:T(8,128)} %broadcast_in_dim.5), calls=%async_computation.7 | async-start | bytes 262144 | tf_op jit(solution)/shard_map/all_to_all | solution.py:34
  197.6 0.9 multiply_convert_fusion
  198.4 8.9 %all-to-all-done.7 = f32[32,8,128]{2,1,0:T(8,128)S(1)} async-done(((f32[32,8,128]{2,1,0:T(8,128)}), f32[32,8,128]{2,1,0:T(8,128)S(1)}, u32[]{:S(2)}, u32[]{:S(2)}) %all-to-all-start.7) | async-done | bytes 131104 | tf_op jit(solution)/shard_map/all_to_all | solution.py:34
  207.3 11.4 %all_gather.11 = f32[4,200,128]{2,1,0:T(8,128)S(1)} all-gather(f32[1,200,128]{2,1,0:T(8,128)S(1)} %slice_bitcast_fusion), channel_id=1, replica_groups=mesh['zq'=4,'zr'=4,'yl'=2,'xh'=2,'xl'=2,'yh'=2,'core'=2] {'xl','core'}, dimensions={0}, use_global_device_ids=true | all-gather | bytes 512000 | tf_op jit(solution)/shard_map/all_gather | solution.py:117
  219.3 0.6 fusion.33
  220.0 0.7 copy-done.3
  (94 shorter events, 15.9 us)
Async XLA Ops:
  0.6 78.6 %copy-start = (bf16[128,128]{1,0:T(8,128)(2,1)S(1)}, bf16[128,128]{1,0:T(8,128)(2,1)}, u32[]{:S(2)}) copy-start(bf16[128,128]{1,0:T(8,128)(2,1)} %param.15) | copy-start | bytes 98308
  0.6 1.2 copy-start.1
  1.8 0.7 copy-start.5
  1.8 0.7 copy-start.6
  2.0 0.9 copy-start.2
  78.4 0.7 copy-start.4
  78.4 0.7 copy-start.7
  79.2 0.9 copy-start.8
  83.1 16.5 %all-to-all-start.2 = ((bf16[128,2,144]{2,1,0:T(2,128)(2,1)}), bf16[128,2,144]{2,1,0:T(2,128)(2,1)S(1)}, u32[]{:S(2)}, u32[]{:S(2)}) async-start(bf16[128,2,144]{2,1,0:T(2,128)(2,1)} %reshape.176), calls=%async_computation.2 | async-start | bytes 262144 | tf_op jit(solution)/shard_map/all_to_all | solution.py:34
  102.5 23.7 %all-to-all-start.3 = ((bf16[4,96,384]{2,1,0:T(8,128)(2,1)}), bf16[4,96,384]{2,1,0:T(8,128)(2,1)S(1)}, u32[]{:S(2)}, u32[]{:S(2)}) async-start(bf16[4,96,384]{2,1,0:T(8,128)(2,1)} %bitcast.18), calls=%async_computation.3 | async-start | bytes 589824 | tf_op jit(solution)/shard_map/all_to_all | solution.py:34
  129.0 21.9 %all-to-all-start.4 = ((bf16[128,2,288]{2,1,0:T(2,128)(2,1)}), bf16[128,2,288]{2,1,0:T(2,128)(2,1)S(1)}, u32[]{:S(2)}, u32[]{:S(2)}) async-start(bf16[128,2,288]{2,1,0:T(2,128)(2,1)} %reshape.178), calls=%async_computation.4 | async-start | bytes 393216 | tf_op jit(solution)/shard_map/all_to_all | solution.py:34
  176.5 8.3 %collective-permute-start = (f32[8,128]{1,0:T(8,128)S(1)}, f32[8,128]{1,0:T(8,128)S(1)}, u32[]{:S(2)}, u32[]{:S(2)}) collective-permute-start(f32[8,128]{1,0:T(8,128)S(1)} %reduce_sum.152), channel_id=1, source_target_pairs={{0,384},{384,0},{128,256},{256,128},{1,385},{385,1},{129,257},{257... | collective-permute-start | bytes 12296 | tf_op jit(solution)/shard_map/ppermute | solution.py:113
  184.8 8.2 %collective-permute-start.1 = (f32[8,128]{1,0:T(8,128)S(1)}, f32[8,128]{1,0:T(8,128)S(1)}, u32[]{:S(2)}, u32[]{:S(2)}) collective-permute-start(f32[8,128]{1,0:T(8,128)S(1)} %add.71), channel_id=1, source_target_pairs={{0,128},{128,0},{256,384},{384,256},{1,129},{129,1},{257,385},{385... | collective-permute-start | bytes 12296 | tf_op jit(solution)/shard_map/ppermute | solution.py:114
  193.7 13.6 %all-to-all-start.7 = ((f32[32,8,128]{2,1,0:T(8,128)}), f32[32,8,128]{2,1,0:T(8,128)S(1)}, u32[]{:S(2)}, u32[]{:S(2)}) async-start(f32[32,8,128]{2,1,0:T(8,128)} %broadcast_in_dim.5), calls=%async_computation.7 | async-start | bytes 262144 | tf_op jit(solution)/shard_map/all_to_all | solution.py:34
  220.0 0.7 copy-start.3

commit v4 on v3

--- a/solution.py
+++ b/solution.py
@@ -4,8 +4,6 @@
 from jax.sharding import Mesh, PartitionSpec as P
 
 CUBE = ("zr", "yl", "xh", "xl", "yh", "core")
-MID = ("zr", "yl", "xh", "yh")
-QUAD = ("xl", "core")
 BF = jnp.bfloat16
 F32 = jnp.float32
 
@@ -105,16 +103,13 @@
     )
     blocks = [dot(in_norm, part, 0, 1) for part in d_proj]
     blocks += [dot(in_norm, d_five, 0, 0), dot(out_norm, d_lin, 1, 0), norms]
-    used, share, slots = 6 * c + 4, 200, 256
-    stacked = jnp.concatenate(blocks + [jnp.zeros((4 * share - used, c), F32)])
-    ours = jnp.sum(exchange(stacked.reshape(4, share, c), QUAD), axis=0)
-    ours = jnp.pad(ours, ((0, slots - share), (0, 0))).reshape(32, slots // 32, c)
-    mine = jnp.sum(exchange(ours, MID), axis=0)
-    mine = mine + lax.ppermute(mine, "zq", [(0, 3), (3, 0), (1, 2), (2, 1)])
-    mine = mine + lax.ppermute(mine, "zq", [(0, 1), (1, 0), (2, 3), (3, 2)])
-    mine = jnp.broadcast_to((mine * (1.0 / all_k))[None], ours.shape)
-    summed = exchange(mine, MID).reshape(slots, c)
-    summed = lax.all_gather(summed[:share], QUAD).reshape(4 * share, c)
+    used, slots = 6 * c + 4, 8
+    stacked = jnp.concatenate(blocks + [jnp.zeros((slots * c - used, c), F32)])
+    mine = jnp.sum(exchange(stacked.reshape(c, slots, c)), axis=0)
+    four = exchange(jnp.broadcast_to(mine[None], (quarters, slots, c)), ("zq",))
+    mine = ((four[0] + four[1]) + (four[2] + four[3])) * (1.0 / all_k)
+    summed = exchange(jnp.broadcast_to(mine.astype(BF)[None], (c, slots, c)))
+    summed = summed.reshape(slots * c, c).astype(F32)
     grad_in = jnp.concatenate([summed[b * c : (b + 1) * c] for b in range(5)], axis=1)
     return (
         pair_out.reshape(ni, nk, c),

time: 221 us -> 216 us (0.977)
  waiting for transfers between devices: 55.1 us -> 49.5 us
  starting transfers between devices: 34 us -> 30.3 us
  blocking collectives: 104 us -> 107 us
    all_to_all x4, blocking collectives: 67.4 us -> 82.2 us  [exchange(): return lax.all_to_all(x, axes, split_axis=0, concat_axis=0, tiled=True)]
    all_gather x1 -> x0, blocking collectives: 11.4 us -> none  [local(): summed = lax.all_gather(summed[:share], QUAD).reshape(4 * share, c)]
    ppermute x2 -> x0, waiting for transfers between devices: 8.72 us -> none  [the longest x1 4.55 us: local(): mine = mine + lax.ppermute(mine, 'zq', [(0, 1), (1, 0), (2, 3), (3, 2)])]
    ppermute x2 -> x0, starting transfers between devices: 7.77 us -> none  [the longest x1 4.08 us: local(): mine = mine + lax.ppermute(mine, 'zq', [(0, 3), (3, 0), (1, 2), (2, 1)])]
    all_to_all x4, starting transfers between devices: 26.2 us -> 30.3 us  [exchange(): return lax.all_to_all(x, axes, split_axis=0, concat_axis=0, tiled=True)]
    all_to_all x4, waiting for transfers between devices: 46.4 us -> 49.5 us  [exchange(): return lax.all_to_all(x, axes, split_axis=0, concat_axis=0, tiled=True)]
  transfers between devices with their start and end apart: 6 -> 4, of which waited for: 6 -> 4; matrix products, arithmetic and copies ran while one was open for 1% -> 1% of each run, Pallas kernels for 0% -> 0%
where the time goes in v4:
time: 216 us; the launch traced here: 215 us
  blocking collectives  107 us (50%)
  waiting for transfers between devices  49.5 us (23%)
  starting transfers between devices  30.3 us (14%)
  local copies, waits for them, and re-layouts  15.8 us (7%)
  other arithmetic  6.35 us (3%)
  matrix products  5.08 us (2%)
    all_to_all x4, blocking collectives, exchange(): return lax.all_to_all(x, axes, split_axis=0, concat_axis=0, tiled=True)  82.2 us
    all_to_all x4, waiting for transfers between devices, exchange(): return lax.all_to_all(x, axes, split_axis=0, concat_axis=0, tiled=True)  49.5 us
    all_to_all x4, starting transfers between devices, exchange(): return lax.all_to_all(x, axes, split_axis=0, concat_axis=0, tiled=True)  30.3 us
    all_gather x1, blocking collectives, local(): lax.all_gather(to_matrix(got[:, pairs:]), 'zq').reshape(all_k, all_k)  24.9 us
    unnamed x30, local copies, waits for them, and re-layouts  5.65 us
    dot_general x15, matrix products, dot(): lax.dot_general(a, b, (((da,), (db,)), ((), ())), preferred_element_type=...  5.08 us
  transfers between devices with their start and end apart: 4, of which 4 were waited for; matrix products, arithmetic and copies ran while one was open for 1% of the time, Pallas kernels for 0%

profile of v4, /device:TPU:1, one launch (start us, length us, event | category | flops | bytes accessed | tf_op | source)
XLA Modules:
  0.0 215.2 jit_solution(16442352005209332788)
XLA Ops:
  0.7 1.1 convert_reduce_fusion
  3.8 0.7 reduce.6
  4.9 25.4 %all_to_all.63 = bf16[128,2,288]{2,1,0:T(2,128)(2,1)S(1)} all-to-all(bf16[128,2,288]{2,1,0:T(2,128)(2,1)S(1)} %reshape.171), channel_id=1, replica_groups=mesh['zq'=4,'zr'=4,'yl'=2,'xh'=2,'xl'=2,'yh'=2,'core'=2] {'zr','yl','xh'..., dimensions={0} | all-to-all | bytes 294912 | tf_op jit(solution)/shard_map/all_to_all | solution.py:32
  31.0 0.6 reshape.150
  32.1 24.9 %all_gather.3 = bf16[4,96,384]{2,1,0:T(8,128)(2,1)S(1)} all-gather(bf16[1,96,384]{2,1,0:T(8,128)(2,1)S(1)} %all_gather_reshape.3), channel_id=1, replica_groups=mesh['zq'=4,'zr'=4,'yl'=2,'xh'=2,'xl'=2,'yh'=2,'core'=2] {'zq'}, dimensions={0}, use_global_device_ids=true | all-gather | bytes 368640 | tf_op jit(solution)/shard_map/all_gather | solution.py:62
  58.5 0.6 all_to_all.54
  59.2 18.7 %all_to_all.64 = f32[128,1,288]{2,1,0:T(1,128)S(1)} all-to-all(f32[128,1,288]{2,1,0:T(1,128)S(1)} %all_to_all.54), channel_id=1, replica_groups=mesh['zq'=4,'zr'=4,'yl'=2,'xh'=2,'xl'=2,'yh'=2,'core'=2] {'zr','yl','xh'..., dimensions={0} | all-to-all | bytes 294912 | tf_op jit(solution)/shard_map/all_to_all | solution.py:32
  78.4 0.6 copy-done.4
  79.4 0.7 copy-done.8
  80.1 0.9 fusion.13
  81.6 0.7 reduce.7
  82.4 0.8 reshape.173
  83.1 5.8 %all-to-all-start.2 = ((bf16[128,2,144]{2,1,0:T(2,128)(2,1)}), bf16[128,2,144]{2,1,0:T(2,128)(2,1)S(1)}, u32[]{:S(2)}, u32[]{:S(2)}) async-start(bf16[128,2,144]{2,1,0:T(2,128)(2,1)} %reshape.173), calls=%async_computation.2 | async-start | bytes 262144 | tf_op jit(solution)/shard_map/all_to_all | solution.py:32
  89.3 10.4 %all-to-all-done.2 = bf16[128,2,144]{2,1,0:T(2,128)(2,1)S(1)} async-done(((bf16[128,2,144]{2,1,0:T(2,128)(2,1)}), bf16[128,2,144]{2,1,0:T(2,128)(2,1)S(1)}, u32[]{:S(2)}, u32[]{:S(2)}) %all-to-all-start.2) | async-done | bytes 73760 | tf_op jit(solution)/shard_map/all_to_all | solution.py:32
  99.8 0.6 reduce.5
  100.4 0.5 reshape.152
  101.5 1.0 convolution_convert_fusion
  102.5 6.4 %all-to-all-start.3 = ((bf16[4,96,384]{2,1,0:T(8,128)(2,1)}), bf16[4,96,384]{2,1,0:T(8,128)(2,1)S(1)}, u32[]{:S(2)}, u32[]{:S(2)}) async-start(bf16[4,96,384]{2,1,0:T(8,128)(2,1)} %bitcast.18), calls=%async_computation.3 | async-start | bytes 589824 | tf_op jit(solution)/shard_map/all_to_all | solution.py:32
  110.1 16.1 %all-to-all-done.3 = bf16[4,96,384]{2,1,0:T(8,128)(2,1)S(1)} async-done(((bf16[4,96,384]{2,1,0:T(8,128)(2,1)}), bf16[4,96,384]{2,1,0:T(8,128)(2,1)S(1)}, u32[]{:S(2)}, u32[]{:S(2)}) %all-to-all-start.3) | async-done | bytes 294944 | tf_op jit(solution)/shard_map/all_to_all | solution.py:32
  127.4 0.7 reduce.8
  128.1 0.9 reshape.175
  129.0 10.2 %all-to-all-start.4 = ((bf16[128,2,288]{2,1,0:T(2,128)(2,1)}), bf16[128,2,288]{2,1,0:T(2,128)(2,1)S(1)}, u32[]{:S(2)}, u32[]{:S(2)}) async-start(bf16[128,2,288]{2,1,0:T(2,128)(2,1)} %reshape.175), calls=%async_computation.4 | async-start | bytes 393216 | tf_op jit(solution)/shard_map/all_to_all | solution.py:32
  139.8 11.1 %all-to-all-done.4 = bf16[128,2,288]{2,1,0:T(2,128)(2,1)S(1)} async-done(((bf16[128,2,288]{2,1,0:T(2,128)(2,1)}), bf16[128,2,288]{2,1,0:T(2,128)(2,1)S(1)}, u32[]{:S(2)}, u32[]{:S(2)}) %all-to-all-start.4) | async-done | bytes 147488 | tf_op jit(solution)/shard_map/all_to_all | solution.py:32
  153.3 23.4 %all_to_all.65 = f32[128,8,128]{2,1,0:T(8,128)S(1)} all-to-all(f32[128,8,128]{2,1,0:T(8,128)S(1)} %bitcast.143), channel_id=1, replica_groups=mesh['zq'=4,'zr'=4,'yl'=2,'xh'=2,'xl'=2,'yh'=2,'core'=2] {'zr','yl','xh'..., dimensions={0} | all-to-all | bytes 1048576 | tf_op jit(solution)/shard_map/all_to_all | solution.py:32
  176.8 14.7 %all_to_all.66 = f32[4,8,128]{2,1,0:T(8,128)S(1)} all-to-all(f32[4,8,128]{2,1,0:T(8,128)S(1)} %broadcast_in_dim.9), channel_id=1, replica_groups=mesh['zq'=4,'zr'=4,'yl'=2,'xh'=2,'xl'=2,'yh'=2,'core'=2] {'zq'}, dimensions={0} | all-to-all | bytes 32768 | tf_op jit(solution)/shard_map/all_to_all | solution.py:32
  191.6 0.7 broadcast_in_dim.11
  192.3 8.0 %all-to-all-start.7 = ((bf16[128,8,128]{2,1,0:T(8,128)(2,1)}), bf16[128,8,128]{2,1,0:T(8,128)(2,1)S(1)}, u32[]{:S(2)}, u32[]{:S(2)}) async-start(bf16[128,8,128]{2,1,0:T(8,128)(2,1)} %broadcast_in_dim.11), calls=%async_computation.7 | async-start | bytes 524288 | tf_op jit(solution)/shard_map/all_to_all | solution.py:32
  200.3 0.9 multiply_convert_fusion
  201.2 11.9 %all-to-all-done.7 = bf16[128,8,128]{2,1,0:T(8,128)(2,1)S(1)} async-done(((bf16[128,8,128]{2,1,0:T(8,128)(2,1)}), bf16[128,8,128]{2,1,0:T(8,128)(2,1)S(1)}, u32[]{:S(2)}, u32[]{:S(2)}) %all-to-all-start.7) | async-done | bytes 262176 | tf_op jit(solution)/shard_map/all_to_all | solution.py:32
  213.2 0.6 slice_bitcast_fusion
  213.8 0.6 slice.127
  214.5 0.7 copy-done.3
  (88 shorter events, 13.4 us)
Async XLA Ops:
  0.6 78.6 %copy-start = (bf16[128,128]{1,0:T(8,128)(2,1)S(1)}, bf16[128,128]{1,0:T(8,128)(2,1)}, u32[]{:S(2)}) copy-start(bf16[128,128]{1,0:T(8,128)(2,1)} %param.15) | copy-start | bytes 98308
  0.6 1.2 copy-start.1
  1.8 0.7 copy-start.5
  1.8 0.7 copy-start.6
  2.0 0.9 copy-start.2
  78.4 0.7 copy-start.4
  78.4 0.7 copy-start.7
  79.2 0.9 copy-start.8
  83.1 16.5 %all-to-all-start.2 = ((bf16[128,2,144]{2,1,0:T(2,128)(2,1)}), bf16[128,2,144]{2,1,0:T(2,128)(2,1)S(1)}, u32[]{:S(2)}, u32[]{:S(2)}) async-start(bf16[128,2,144]{2,1,0:T(2,128)(2,1)} %reshape.173), calls=%async_computation.2 | async-start | bytes 262144 | tf_op jit(solution)/shard_map/all_to_all | solution.py:32
  102.5 23.7 %all-to-all-start.3 = ((bf16[4,96,384]{2,1,0:T(8,128)(2,1)}), bf16[4,96,384]{2,1,0:T(8,128)(2,1)S(1)}, u32[]{:S(2)}, u32[]{:S(2)}) async-start(bf16[4,96,384]{2,1,0:T(8,128)(2,1)} %bitcast.18), calls=%async_computation.3 | async-start | bytes 589824 | tf_op jit(solution)/shard_map/all_to_all | solution.py:32
  129.0 21.9 %all-to-all-start.4 = ((bf16[128,2,288]{2,1,0:T(2,128)(2,1)}), bf16[128,2,288]{2,1,0:T(2,128)(2,1)S(1)}, u32[]{:S(2)}, u32[]{:S(2)}) async-start(bf16[128,2,288]{2,1,0:T(2,128)(2,1)} %reshape.175), calls=%async_computation.4 | async-start | bytes 393216 | tf_op jit(solution)/shard_map/all_to_all | solution.py:32
  192.3 20.8 %all-to-all-start.7 = ((bf16[128,8,128]{2,1,0:T(8,128)(2,1)}), bf16[128,8,128]{2,1,0:T(8,128)(2,1)S(1)}, u32[]{:S(2)}, u32[]{:S(2)}) async-start(bf16[128,8,128]{2,1,0:T(8,128)(2,1)} %broadcast_in_dim.11), calls=%async_computation.7 | async-start | bytes 524288 | tf_op jit(solution)/shard_map/all_to_all | solution.py:32
  214.5 0.7 copy-start.3

commit v5 on v4

--- a/solution.py
+++ b/solution.py
@@ -4,6 +4,7 @@
 from jax.sharding import Mesh, PartitionSpec as P
 
 CUBE = ("zr", "yl", "xh", "xl", "yh", "core")
+CHIPS = ("zr", "yl", "xh", "xl", "yh")
 BF = jnp.bfloat16
 F32 = jnp.float32
 
@@ -103,13 +104,13 @@
     )
     blocks = [dot(in_norm, part, 0, 1) for part in d_proj]
     blocks += [dot(in_norm, d_five, 0, 0), dot(out_norm, d_lin, 1, 0), norms]
-    used, slots = 6 * c + 4, 8
-    stacked = jnp.concatenate(blocks + [jnp.zeros((slots * c - used, c), F32)])
-    mine = jnp.sum(exchange(stacked.reshape(c, slots, c)), axis=0)
-    four = exchange(jnp.broadcast_to(mine[None], (quarters, slots, c)), ("zq",))
-    mine = ((four[0] + four[1]) + (four[2] + four[3])) * (1.0 / all_k)
-    summed = exchange(jnp.broadcast_to(mine.astype(BF)[None], (c, slots, c)))
-    summed = summed.reshape(slots * c, c).astype(F32)
+    used, slots, peers = 6 * c + 4, 16, c // 2
+    stacked = jnp.concatenate(blocks + [jnp.zeros((slots * peers - used, c), F32)]).astype(BF)
+    mine = jnp.sum(exchange(stacked.reshape(peers, slots, c), CHIPS).astype(F32), axis=0)
+    eight = exchange(jnp.broadcast_to(mine[None], (2 * quarters, slots, c)), ("zq", "core"))
+    mine = (jnp.sum(eight, axis=0) * (1.0 / all_k)).astype(BF)
+    summed = exchange(jnp.broadcast_to(mine[None], (peers, slots, c)), CHIPS)
+    summed = summed.reshape(slots * peers, c).astype(F32)
     grad_in = jnp.concatenate([summed[b * c : (b + 1) * c] for b in range(5)], axis=1)
     return (
         pair_out.reshape(ni, nk, c),

time: 216 us -> 207 us (0.958)
  blocking collectives: 107 us -> 102 us
  waiting for transfers between devices: 49.5 us -> 46.5 us
  starting transfers between devices: 30.3 us -> 27.6 us
    all_to_all x4, blocking collectives: 82.2 us -> 77.5 us  [exchange(): return lax.all_to_all(x, axes, split_axis=0, concat_axis=0, tiled=True)]
    all_to_all x4, waiting for transfers between devices: 49.5 us -> 46.5 us  [exchange(): return lax.all_to_all(x, axes, split_axis=0, concat_axis=0, tiled=True)]
    all_to_all x4, starting transfers between devices: 30.3 us -> 27.6 us  [exchange(): return lax.all_to_all(x, axes, split_axis=0, concat_axis=0, tiled=True)]
  transfers between devices with their start and end apart: 4 -> 4, of which waited for: 4 -> 4; matrix products, arithmetic and copies ran while one was open for 1% -> 2% of each run, Pallas kernels for 0% -> 0%
where the time goes in v5:
time: 207 us; the launch traced here: 205 us
  blocking collectives  102 us (49%)
  waiting for transfers between devices  46.5 us (22%)
  starting transfers between devices  27.6 us (13%)
  local copies, waits for them, and re-layouts  15.9 us (8%)
  other arithmetic  6.26 us (3%)
  matrix products  5.1 us (2%)
    all_to_all x4, blocking collectives, exchange(): return lax.all_to_all(x, axes, split_axis=0, concat_axis=0, tiled=True)  77.5 us
    all_to_all x4, waiting for transfers between devices, exchange(): return lax.all_to_all(x, axes, split_axis=0, concat_axis=0, tiled=True)  46.5 us
    all_to_all x4, starting transfers between devices, exchange(): return lax.all_to_all(x, axes, split_axis=0, concat_axis=0, tiled=True)  27.6 us
    all_gather x1, blocking collectives, local(): lax.all_gather(to_matrix(got[:, pairs:]), 'zq').reshape(all_k, all_k)  24.9 us
    unnamed x30, local copies, waits for them, and re-layouts  5.65 us
    dot_general x15, matrix products, dot(): lax.dot_general(a, b, (((da,), (db,)), ((), ())), preferred_element_type=...  5.1 us
  transfers between devices with their start and end apart: 4, of which 4 were waited for; matrix products, arithmetic and copies ran while one was open for 2% of the time, Pallas kernels for 0%

profile of v5, /device:TPU:1, one launch (start us, length us, event | category | flops | bytes accessed | tf_op | source)
XLA Modules:
  0.0 205.0 jit_solution(12407481698242548805)
XLA Ops:
  0.7 1.1 convert_reduce_fusion.1
  3.8 0.7 reduce.6
  4.9 25.4 %all_to_all.63 = bf16[128,2,288]{2,1,0:T(2,128)(2,1)S(1)} all-to-all(bf16[128,2,288]{2,1,0:T(2,128)(2,1)S(1)} %reshape.174), channel_id=1, replica_groups=mesh['zq'=4,'zr'=4,'yl'=2,'xh'=2,'xl'=2,'yh'=2,'core'=2] {'zr','yl','xh'..., dimensions={0} | all-to-all | bytes 294912 | tf_op jit(solution)/shard_map/all_to_all | solution.py:33
  31.0 0.6 reshape.154
  32.1 24.9 %all_gather.3 = bf16[4,96,384]{2,1,0:T(8,128)(2,1)S(1)} all-gather(bf16[1,96,384]{2,1,0:T(8,128)(2,1)S(1)} %all_gather_reshape.3), channel_id=1, replica_groups=mesh['zq'=4,'zr'=4,'yl'=2,'xh'=2,'xl'=2,'yh'=2,'core'=2] {'zq'}, dimensions={0}, use_global_device_ids=true | all-gather | bytes 368640 | tf_op jit(solution)/shard_map/all_gather | solution.py:63
  56.9 0.5 reshape.153
  58.5 0.6 all_to_all.54
  59.2 18.7 %all_to_all.64 = f32[128,1,288]{2,1,0:T(1,128)S(1)} all-to-all(f32[128,1,288]{2,1,0:T(1,128)S(1)} %all_to_all.54), channel_id=1, replica_groups=mesh['zq'=4,'zr'=4,'yl'=2,'xh'=2,'xl'=2,'yh'=2,'core'=2] {'zr','yl','xh'..., dimensions={0} | all-to-all | bytes 294912 | tf_op jit(solution)/shard_map/all_to_all | solution.py:33
  78.4 0.6 copy-done.4
  79.4 0.7 copy-done.8
  80.1 0.9 fusion.13
  81.6 0.7 reduce.7
  82.4 0.8 reshape.176
  83.1 5.8 %all-to-all-start.2 = ((bf16[128,2,144]{2,1,0:T(2,128)(2,1)}), bf16[128,2,144]{2,1,0:T(2,128)(2,1)S(1)}, u32[]{:S(2)}, u32[]{:S(2)}) async-start(bf16[128,2,144]{2,1,0:T(2,128)(2,1)} %reshape.176), calls=%async_computation.2 | async-start | bytes 262144 | tf_op jit(solution)/shard_map/all_to_all | solution.py:33
  89.3 10.4 %all-to-all-done.2 = bf16[128,2,144]{2,1,0:T(2,128)(2,1)S(1)} async-done(((bf16[128,2,144]{2,1,0:T(2,128)(2,1)}), bf16[128,2,144]{2,1,0:T(2,128)(2,1)S(1)}, u32[]{:S(2)}, u32[]{:S(2)}) %all-to-all-start.2) | async-done | bytes 73760 | tf_op jit(solution)/shard_map/all_to_all | solution.py:33
  99.8 0.6 reduce.5
  101.5 1.0 convolution_convert_fusion
  102.5 6.4 %all-to-all-start.3 = ((bf16[4,96,384]{2,1,0:T(8,128)(2,1)}), bf16[4,96,384]{2,1,0:T(8,128)(2,1)S(1)}, u32[]{:S(2)}, u32[]{:S(2)}) async-start(bf16[4,96,384]{2,1,0:T(8,128)(2,1)} %bitcast.18), calls=%async_computation.3 | async-start | bytes 589824 | tf_op jit(solution)/shard_map/all_to_all | solution.py:33
  110.1 16.1 %all-to-all-done.3 = bf16[4,96,384]{2,1,0:T(8,128)(2,1)S(1)} async-done(((bf16[4,96,384]{2,1,0:T(8,128)(2,1)}), bf16[4,96,384]{2,1,0:T(8,128)(2,1)S(1)}, u32[]{:S(2)}, u32[]{:S(2)}) %all-to-all-start.3) | async-done | bytes 294944 | tf_op jit(solution)/shard_map/all_to_all | solution.py:33
  127.4 0.7 reduce.8
  128.1 0.9 reshape.178
  129.0 10.2 %all-to-all-start.4 = ((bf16[128,2,288]{2,1,0:T(2,128)(2,1)}), bf16[128,2,288]{2,1,0:T(2,128)(2,1)S(1)}, u32[]{:S(2)}, u32[]{:S(2)}) async-start(bf16[128,2,288]{2,1,0:T(2,128)(2,1)} %reshape.178), calls=%async_computation.4 | async-start | bytes 393216 | tf_op jit(solution)/shard_map/all_to_all | solution.py:33
  139.8 11.1 %all-to-all-done.4 = bf16[128,2,288]{2,1,0:T(2,128)(2,1)S(1)} async-done(((bf16[128,2,288]{2,1,0:T(2,128)(2,1)}), bf16[128,2,288]{2,1,0:T(2,128)(2,1)S(1)}, u32[]{:S(2)}, u32[]{:S(2)}) %all-to-all-start.4) | async-done | bytes 147488 | tf_op jit(solution)/shard_map/all_to_all | solution.py:33
  153.4 14.4 %all_to_all.65 = bf16[64,16,128]{2,1,0:T(8,128)(2,1)S(1)} all-to-all(bf16[64,16,128]{2,1,0:T(8,128)(2,1)S(1)} %bitcast.133), channel_id=1, replica_groups=mesh['zq'=4,'zr'=4,'yl'=2,'xh'=2,'xl'=2,'yh'=2,'core'=2] {'zr','yl','xh'..., dimensions={0} | all-to-all | bytes 524288 | tf_op jit(solution)/shard_map/all_to_all | solution.py:33
  167.9 19.1 %all_to_all.66 = f32[8,16,128]{2,1,0:T(8,128)S(1)} all-to-all(f32[8,16,128]{2,1,0:T(8,128)S(1)} %broadcast_in_dim.7), channel_id=1, replica_groups=mesh['zq'=4,'zr'=4,'yl'=2,'xh'=2,'xl'=2,'yh'=2,'core'=2] {'zq','core'}, dimensions={0} | all-to-all | bytes 131072 | tf_op jit(solution)/shard_map/all_to_all | solution.py:33
  187.0 0.7 broadcast_in_dim.8
  187.8 5.3 %all-to-all-start.7 = ((bf16[64,16,128]{2,1,0:T(8,128)(2,1)}), bf16[64,16,128]{2,1,0:T(8,128)(2,1)S(1)}, u32[]{:S(2)}, u32[]{:S(2)}) async-start(bf16[64,16,128]{2,1,0:T(8,128)(2,1)} %broadcast_in_dim.8), calls=%async_computation.7 | async-start | bytes 524288 | tf_op jit(solution)/shard_map/all_to_all | solution.py:33
  193.1 0.9 multiply_convert_fusion
  193.9 9.0 %all-to-all-done.7 = bf16[64,16,128]{2,1,0:T(8,128)(2,1)S(1)} async-done(((bf16[64,16,128]{2,1,0:T(8,128)(2,1)}), bf16[64,16,128]{2,1,0:T(8,128)(2,1)S(1)}, u32[]{:S(2)}, u32[]{:S(2)}) %all-to-all-start.7) | async-done | bytes 262176 | tf_op jit(solution)/shard_map/all_to_all | solution.py:33
  203.0 0.6 slice.107
  203.5 0.7 fusion.33
  204.3 0.7 copy-done.3
  (89 shorter events, 13.4 us)
Async XLA Ops:
  0.6 78.6 %copy-start = (bf16[128,128]{1,0:T(8,128)(2,1)S(1)}, bf16[128,128]{1,0:T(8,128)(2,1)}, u32[]{:S(2)}) copy-start(bf16[128,128]{1,0:T(8,128)(2,1)} %param.15) | copy-start | bytes 98308
  0.6 1.2 copy-start.1
  1.8 0.7 copy-start.5
  1.8 0.7 copy-start.6
  2.0 0.9 copy-start.2
  78.4 0.7 copy-start.4
  78.4 0.7 copy-start.7
  79.2 0.9 copy-start.8
  83.1 16.5 %all-to-all-start.2 = ((bf16[128,2,144]{2,1,0:T(2,128)(2,1)}), bf16[128,2,144]{2,1,0:T(2,128)(2,1)S(1)}, u32[]{:S(2)}, u32[]{:S(2)}) async-start(bf16[128,2,144]{2,1,0:T(2,128)(2,1)} %reshape.176), calls=%async_computation.2 | async-start | bytes 262144 | tf_op jit(solution)/shard_map/all_to_all | solution.py:33
  102.5 23.7 %all-to-all-start.3 = ((bf16[4,96,384]{2,1,0:T(8,128)(2,1)}), bf16[4,96,384]{2,1,0:T(8,128)(2,1)S(1)}, u32[]{:S(2)}, u32[]{:S(2)}) async-start(bf16[4,96,384]{2,1,0:T(8,128)(2,1)} %bitcast.18), calls=%async_computation.3 | async-start | bytes 589824 | tf_op jit(solution)/shard_map/all_to_all | solution.py:33
  129.0 21.9 %all-to-all-start.4 = ((bf16[128,2,288]{2,1,0:T(2,128)(2,1)}), bf16[128,2,288]{2,1,0:T(2,128)(2,1)S(1)}, u32[]{:S(2)}, u32[]{:S(2)}) async-start(bf16[128,2,288]{2,1,0:T(2,128)(2,1)} %reshape.178), calls=%async_computation.4 | async-start | bytes 393216 | tf_op jit(solution)/shard_map/all_to_all | solution.py:33
  187.8 15.2 %all-to-all-start.7 = ((bf16[64,16,128]{2,1,0:T(8,128)(2,1)}), bf16[64,16,128]{2,1,0:T(8,128)(2,1)S(1)}, u32[]{:S(2)}, u32[]{:S(2)}) async-start(bf16[64,16,128]{2,1,0:T(8,128)(2,1)} %broadcast_in_dim.8), calls=%async_computation.7 | async-start | bytes 524288 | tf_op jit(solution)/shard_map/all_to_all | solution.py:33
  204.3 0.7 copy-start.3

commit v6 on v5

--- a/solution.py
+++ b/solution.py
@@ -40,7 +40,7 @@
     rows, all_k = rr * ni, cols * nk
 
     def to_matrix(x):
-        x = x.reshape(rr, cols, ni, nk).transpose(0, 2, 1, 3)
+        x = x.reshape(rr, cols, 2, ni // 2, nk).transpose(0, 2, 3, 1, 4)
         return x.reshape(rows, all_k)
 
     def from_matrix(x):
@@ -58,9 +58,9 @@
     left = (left_sig * lin_left).astype(BF)
     right = (right_sig * lin_right).astype(BF)
 
-    got = exchange(jnp.concatenate([left, right], axis=1))
-    left_own = to_matrix(got[:, :pairs])
-    right_all = lax.all_gather(to_matrix(got[:, pairs:]), "zq").reshape(all_k, all_k)
+    got = exchange(jnp.stack([left, right], axis=1))
+    left_own = to_matrix(got[:, 0])
+    right_all = lax.all_gather(to_matrix(got[:, 1]), "zq").reshape(all_k, all_k)
     product = dot(left_own, right_all, 1, 1)
     prod = exchange(from_matrix(product))
 
@@ -75,14 +75,14 @@
     d_outnorm = dot(out_weights, d_lin, 1, 1)
     d_product = back(d_outnorm, out_hat, out_rstd, gain_col, 0).astype(BF)
 
-    d_mat = to_matrix(exchange(d_product))
+    d_mat = to_matrix(exchange(d_product.reshape(c, 2, pairs // 2)))
     d_left_m = dot(d_mat, right_all, 1, 0).astype(BF)
     terms = dot(d_mat, left_own, 0, 0).astype(BF)
     terms = exchange(terms.reshape(quarters, rows, all_k), ("zq",))
     d_right_m = jnp.sum(terms.astype(F32), axis=0).astype(BF)
-    d_both = exchange(jnp.concatenate([from_matrix(d_left_m), from_matrix(d_right_m)], axis=1))
+    d_both = exchange(jnp.stack([from_matrix(d_left_m), from_matrix(d_right_m)], axis=1))
     d_both = d_both.astype(F32)
-    d_left, d_right = d_both[:, :pairs], d_both[:, pairs:]
+    d_left, d_right = d_both[:, 0], d_both[:, 1]
 
     d_proj = [
         (d_left * left_sig).astype(BF),

time: 207 us -> 203 us (0.981)
  other arithmetic: 6.26 us -> 3.56 us
    another operation x1 -> x7, local copies, waits for them, and re-layouts: 0.37 us -> 3.36 us  [the longest x3 1.69 us: local(): jnp.stack([from_matrix(d_left_m), from_matrix(d_right_m)], axis=1)]
    all_to_all x7 -> x0, other arithmetic: 2.98 us -> none  [exchange(): return lax.all_to_all(x, axes, split_axis=0, concat_axis=0, tiled=True)]
    unnamed x30 -> x22, local copies, waits for them, and re-layouts: 5.65 us -> 2.8 us
where the time goes in v6:
time: 203 us; the launch traced here: 201 us
  blocking collectives  102 us (50%)
  waiting for transfers between devices  46.5 us (23%)
  starting transfers between devices  27.6 us (14%)
  local copies, waits for them, and re-layouts  14.7 us (7%)
  matrix products  5.11 us (3%)
  other arithmetic  3.56 us (2%)
    all_to_all x4, blocking collectives, exchange(): return lax.all_to_all(x, axes, split_axis=0, concat_axis=0, tiled=True)  77.5 us
    all_to_all x4, waiting for transfers between devices, exchange(): return lax.all_to_all(x, axes, split_axis=0, concat_axis=0, tiled=True)  46.5 us
    all_to_all x4, starting transfers between devices, exchange(): return lax.all_to_all(x, axes, split_axis=0, concat_axis=0, tiled=True)  27.6 us
    all_gather x1, blocking collectives, local(): right_all = lax.all_gather(to_matrix(got[:, 1]), 'zq').reshape(all_k, all_k)  24.9 us
    dot_general x15, matrix products, dot(): lax.dot_general(a, b, (((da,), (db,)), ((), ())), preferred_element_type=...  5.11 us
  transfers between devices with their start and end apart: 4, of which 4 were waited for; matrix products, arithmetic and copies ran while one was open for 2% of the time, Pallas kernels for 0%

profile of v6, /device:TPU:1, one launch (start us, length us, event | category | flops | bytes accessed | tf_op | source)
XLA Modules:
  0.0 201.0 jit_solution(8645374909996045208)
XLA Ops:
  0.7 1.1 convert_reduce_fusion.1
  3.5 25.3 %all_to_all.48 = bf16[128,2,288]{2,1,0:T(2,128)(2,1)S(1)} all-to-all(bf16[128,2,288]{2,1,0:T(2,128)(2,1)S(1)} %copy.43), channel_id=1, replica_groups=mesh['zq'=4,'zr'=4,'yl'=2,'xh'=2,'xl'=2,'yh'=2,'core'=2] {'zr','yl','xh'..., dimensions={0} | all-to-all | bytes 294912 | tf_op jit(solution)/shard_map/all_to_all | solution.py:33
  28.9 1.0 slice_reduce_fusion.1
  29.9 0.6 reshape_squeeze.6
  30.9 0.6 reshape_squeeze.7
  32.0 24.9 %all_gather.3 = bf16[4,96,384]{2,1,0:T(8,128)(2,1)S(1)} all-gather(bf16[1,96,384]{2,1,0:T(8,128)(2,1)S(1)} %all_gather_reshape.3), channel_id=1, replica_groups=mesh['zq'=4,'zr'=4,'yl'=2,'xh'=2,'xl'=2,'yh'=2,'core'=2] {'zq'}, dimensions={0}, use_global_device_ids=true | all-gather | bytes 368640 | tf_op jit(solution)/shard_map/all_gather | solution.py:63
  56.9 0.5 convolution_bitcast_fusion
  57.4 0.6 all_to_all.39
  58.0 18.7 %all_to_all.49 = f32[128,1,288]{2,1,0:T(1,128)S(1)} all-to-all(f32[128,1,288]{2,1,0:T(1,128)S(1)} %all_to_all.39), channel_id=1, replica_groups=mesh['zq'=4,'zr'=4,'yl'=2,'xh'=2,'xl'=2,'yh'=2,'core'=2] {'zr','yl','xh'..., dimensions={0} | all-to-all | bytes 294912 | tf_op jit(solution)/shard_map/all_to_all | solution.py:33
  77.3 0.6 copy-done.4
  78.3 0.7 copy-done.8
  79.0 0.9 fusion.13
  80.4 0.8 copy.49
  81.2 5.8 %all-to-all-start.2 = ((bf16[128,2,144]{2,1,0:T(2,128)(2,1)}), bf16[128,2,144]{2,1,0:T(2,128)(2,1)S(1)}, u32[]{:S(2)}, u32[]{:S(2)}) async-start(bf16[128,2,144]{2,1,0:T(2,128)(2,1)} %copy.49), calls=%async_computation.2 | async-start | bytes 262144 | tf_op jit(solution)/shard_map/all_to_all | solution.py:33
  87.4 10.4 %all-to-all-done.2 = bf16[128,2,144]{2,1,0:T(2,128)(2,1)S(1)} async-done(((bf16[128,2,144]{2,1,0:T(2,128)(2,1)}), bf16[128,2,144]{2,1,0:T(2,128)(2,1)S(1)}, u32[]{:S(2)}, u32[]{:S(2)}) %all-to-all-start.2) | async-done | bytes 73760 | tf_op jit(solution)/shard_map/all_to_all | solution.py:33
  98.6 1.0 convolution_convert_fusion
  99.5 6.4 %all-to-all-start.3 = ((bf16[4,96,384]{2,1,0:T(8,128)(2,1)}), bf16[4,96,384]{2,1,0:T(8,128)(2,1)S(1)}, u32[]{:S(2)}, u32[]{:S(2)}) async-start(bf16[4,96,384]{2,1,0:T(8,128)(2,1)} %bitcast.18), calls=%async_computation.3 | async-start | bytes 589824 | tf_op jit(solution)/shard_map/all_to_all | solution.py:33
  106.2 0.5 reshape.140
  107.2 16.1 %all-to-all-done.3 = bf16[4,96,384]{2,1,0:T(8,128)(2,1)S(1)} async-done(((bf16[4,96,384]{2,1,0:T(8,128)(2,1)}), bf16[4,96,384]{2,1,0:T(8,128)(2,1)S(1)}, u32[]{:S(2)}, u32[]{:S(2)}) %all-to-all-start.3) | async-done | bytes 294944 | tf_op jit(solution)/shard_map/all_to_all | solution.py:33
  124.4 0.9 copy.55
  125.3 10.2 %all-to-all-start.4 = ((bf16[128,2,288]{2,1,0:T(2,128)(2,1)}), bf16[128,2,288]{2,1,0:T(2,128)(2,1)S(1)}, u32[]{:S(2)}, u32[]{:S(2)}) async-start(bf16[128,2,288]{2,1,0:T(2,128)(2,1)} %copy.55), calls=%async_computation.4 | async-start | bytes 393216 | tf_op jit(solution)/shard_map/all_to_all | solution.py:33
  136.1 11.1 %all-to-all-done.4 = bf16[128,2,288]{2,1,0:T(2,128)(2,1)S(1)} async-done(((bf16[128,2,288]{2,1,0:T(2,128)(2,1)}), bf16[128,2,288]{2,1,0:T(2,128)(2,1)S(1)}, u32[]{:S(2)}, u32[]{:S(2)}) %all-to-all-start.4) | async-done | bytes 147488 | tf_op jit(solution)/shard_map/all_to_all | solution.py:33
  148.9 0.5 concatenate.11
  149.4 14.4 %all_to_all.50 = bf16[64,16,128]{2,1,0:T(8,128)(2,1)S(1)} all-to-all(bf16[64,16,128]{2,1,0:T(8,128)(2,1)S(1)} %bitcast.138), channel_id=1, replica_groups=mesh['zq'=4,'zr'=4,'yl'=2,'xh'=2,'xl'=2,'yh'=2,'core'=2] {'zr','yl','xh'..., dimensions={0} | all-to-all | bytes 524288 | tf_op jit(solution)/shard_map/all_to_all | solution.py:33
  163.9 19.1 %all_to_all.51 = f32[8,16,128]{2,1,0:T(8,128)S(1)} all-to-all(f32[8,16,128]{2,1,0:T(8,128)S(1)} %broadcast_in_dim.7), channel_id=1, replica_groups=mesh['zq'=4,'zr'=4,'yl'=2,'xh'=2,'xl'=2,'yh'=2,'core'=2] {'zq','core'}, dimensions={0} | all-to-all | bytes 131072 | tf_op jit(solution)/shard_map/all_to_all | solution.py:33
  183.1 0.7 broadcast_in_dim.8
  183.8 5.3 %all-to-all-start.7 = ((bf16[64,16,128]{2,1,0:T(8,128)(2,1)}), bf16[64,16,128]{2,1,0:T(8,128)(2,1)S(1)}, u32[]{:S(2)}, u32[]{:S(2)}) async-start(bf16[64,16,128]{2,1,0:T(8,128)(2,1)} %broadcast_in_dim.8), calls=%async_computation.7 | async-start | bytes 524288 | tf_op jit(solution)/shard_map/all_to_all | solution.py:33
  189.1 0.9 multiply_convert_fusion
  190.0 9.0 %all-to-all-done.7 = bf16[64,16,128]{2,1,0:T(8,128)(2,1)S(1)} async-done(((bf16[64,16,128]{2,1,0:T(8,128)(2,1)}), bf16[64,16,128]{2,1,0:T(8,128)(2,1)S(1)}, u32[]{:S(2)}, u32[]{:S(2)}) %all-to-all-start.7) | async-done | bytes 262176 | tf_op jit(solution)/shard_map/all_to_all | solution.py:33
  199.0 0.6 slice.107
  199.6 0.7 fusion.34
  200.3 0.7 copy-done.3
  (77 shorter events, 9.5 us)
Async XLA Ops:
  0.6 77.5 %copy-start = (bf16[128,128]{1,0:T(8,128)(2,1)S(1)}, bf16[128,128]{1,0:T(8,128)(2,1)}, u32[]{:S(2)}) copy-start(bf16[128,128]{1,0:T(8,128)(2,1)} %param.15) | copy-start | bytes 98308
  0.6 1.2 copy-start.1
  1.8 0.7 copy-start.5
  1.8 0.7 copy-start.6
  2.0 0.9 copy-start.2
  77.3 0.7 copy-start.4
  77.3 0.7 copy-start.7
  78.1 0.9 copy-start.8
  81.2 16.5 %all-to-all-start.2 = ((bf16[128,2,144]{2,1,0:T(2,128)(2,1)}), bf16[128,2,144]{2,1,0:T(2,128)(2,1)S(1)}, u32[]{:S(2)}, u32[]{:S(2)}) async-start(bf16[128,2,144]{2,1,0:T(2,128)(2,1)} %copy.49), calls=%async_computation.2 | async-start | bytes 262144 | tf_op jit(solution)/shard_map/all_to_all | solution.py:33
  99.5 23.7 %all-to-all-start.3 = ((bf16[4,96,384]{2,1,0:T(8,128)(2,1)}), bf16[4,96,384]{2,1,0:T(8,128)(2,1)S(1)}, u32[]{:S(2)}, u32[]{:S(2)}) async-start(bf16[4,96,384]{2,1,0:T(8,128)(2,1)} %bitcast.18), calls=%async_computation.3 | async-start | bytes 589824 | tf_op jit(solution)/shard_map/all_to_all | solution.py:33
  125.3 21.9 %all-to-all-start.4 = ((bf16[128,2,288]{2,1,0:T(2,128)(2,1)}), bf16[128,2,288]{2,1,0:T(2,128)(2,1)S(1)}, u32[]{:S(2)}, u32[]{:S(2)}) async-start(bf16[128,2,288]{2,1,0:T(2,128)(2,1)} %copy.55), calls=%async_computation.4 | async-start | bytes 393216 | tf_op jit(solution)/shard_map/all_to_all | solution.py:33
  183.8 15.1 %all-to-all-start.7 = ((bf16[64,16,128]{2,1,0:T(8,128)(2,1)}), bf16[64,16,128]{2,1,0:T(8,128)(2,1)S(1)}, u32[]{:S(2)}, u32[]{:S(2)}) async-start(bf16[64,16,128]{2,1,0:T(8,128)(2,1)} %broadcast_in_dim.8), calls=%async_computation.7 | async-start | bytes 524288 | tf_op jit(solution)/shard_map/all_to_all | solution.py:33
  200.3 0.7 copy-start.3

commit v7 on v6

--- a/solution.py
+++ b/solution.py
@@ -62,6 +62,10 @@
     left_own = to_matrix(got[:, 0])
     right_all = lax.all_gather(to_matrix(got[:, 1]), "zq").reshape(all_k, all_k)
     product = dot(left_own, right_all, 1, 1)
+    upstream = cotangent.reshape(pairs, c).astype(F32)
+    d_lin = (upstream * gate).astype(BF)
+    d_outnorm = dot(out_weights, d_lin, 1, 1)
+    product, d_outnorm = lax.optimization_barrier((product, d_outnorm))
     prod = exchange(from_matrix(product))
 
     out_hat, out_rstd = stats(prod, 0)
@@ -69,10 +73,7 @@
     out_norm = (out_hat * gain_col + out_bias[:, None]).astype(BF)
     out_lin = dot(out_norm, out_weights, 0, 0)
     pair_out = (gate * out_lin).astype(BF)
-    upstream = cotangent.reshape(pairs, c).astype(F32)
-    d_lin = (upstream * gate).astype(BF)
     d_gate = upstream * out_lin
-    d_outnorm = dot(out_weights, d_lin, 1, 1)
     d_product = back(d_outnorm, out_hat, out_rstd, gain_col, 0).astype(BF)
 
     d_mat = to_matrix(exchange(d_product.reshape(c, 2, pairs // 2)))

time: 203 us -> 202 us (level)
  blocking collectives: 102 us -> 92.9 us
  starting transfers between devices: 27.6 us -> 35.9 us
    all_to_all x4, blocking collectives: 77.5 us -> 68 us  [exchange(): return lax.all_to_all(x, axes, split_axis=0, concat_axis=0, tiled=True)]
    all_to_all x4, starting transfers between devices: 27.6 us -> 35.9 us  [exchange(): return lax.all_to_all(x, axes, split_axis=0, concat_axis=0, tiled=True)]
where the time goes in v7:
time: 202 us; the launch traced here: 200 us
  blocking collectives  92.9 us (46%)
  waiting for transfers between devices  46.1 us (23%)
  starting transfers between devices  35.9 us (18%)
  local copies, waits for them, and re-layouts  14.9 us (7%)
  matrix products  5.28 us (3%)
  other arithmetic  3.64 us (2%)
    all_to_all x4, blocking collectives, exchange(): return lax.all_to_all(x, axes, split_axis=0, concat_axis=0, tiled=True)  68 us
    all_to_all x4, waiting for transfers between devices, exchange(): return lax.all_to_all(x, axes, split_axis=0, concat_axis=0, tiled=True)  46.1 us
    all_to_all x4, starting transfers between devices, exchange(): return lax.all_to_all(x, axes, split_axis=0, concat_axis=0, tiled=True)  35.9 us
    all_gather x1, blocking collectives, local(): right_all = lax.all_gather(to_matrix(got[:, 1]), 'zq').reshape(all_k, all_k)  24.9 us
    dot_general x15, matrix products, dot(): lax.dot_general(a, b, (((da,), (db,)), ((), ())), preferred_element_type=...  5.28 us
  transfers between devices with their start and end apart: 4, of which 4 were waited for; matrix products, arithmetic and copies ran while one was open for 2% of the time, Pallas kernels for 0%

profile of v7, /device:TPU:1, one launch (start us, length us, event | category | flops | bytes accessed | tf_op | source)
XLA Modules:
  0.0 199.9 jit_solution(7165389101314887939)
XLA Ops:
  0.7 1.1 convert_reduce_fusion.1
  3.3 0.8 copy.40
  4.2 14.0 %all-to-all-start = ((bf16[128,2,288]{2,1,0:T(2,128)(2,1)}), bf16[128,2,288]{2,1,0:T(2,128)(2,1)S(1)}, u32[]{:S(2)}, u32[]{:S(2)}) async-start(bf16[128,2,288]{2,1,0:T(2,128)(2,1)} %copy.40), calls=%async_computation | async-start | bytes 393216 | tf_op jit(solution)/shard_map/all_to_all | solution.py:33
  18.1 0.8 fusion.10
  19.1 10.7 %all-to-all-done = bf16[128,2,288]{2,1,0:T(2,128)(2,1)S(1)} async-done(((bf16[128,2,288]{2,1,0:T(2,128)(2,1)}), bf16[128,2,288]{2,1,0:T(2,128)(2,1)S(1)}, u32[]{:S(2)}, u32[]{:S(2)}) %all-to-all-start) | async-done | bytes 147488 | tf_op jit(solution)/shard_map/all_to_all | solution.py:33
  29.8 1.0 slice_reduce_fusion
  30.8 0.6 reshape_squeeze.6
  31.9 0.6 reshape_squeeze.7
  32.9 24.9 %all_gather.3 = bf16[4,96,384]{2,1,0:T(8,128)(2,1)S(1)} all-gather(bf16[1,96,384]{2,1,0:T(8,128)(2,1)S(1)} %all_gather_reshape.3), channel_id=1, replica_groups=mesh['zq'=4,'zr'=4,'yl'=2,'xh'=2,'xl'=2,'yh'=2,'core'=2] {'zq'}, dimensions={0}, use_global_device_ids=true | all-gather | bytes 368640 | tf_op jit(solution)/shard_map/all_gather | solution.py:63
  58.8 0.6 all_to_all.39
  59.4 18.7 %all_to_all.48 = f32[128,1,288]{2,1,0:T(1,128)S(1)} all-to-all(f32[128,1,288]{2,1,0:T(1,128)S(1)} %all_to_all.39), channel_id=1, replica_groups=mesh['zq'=4,'zr'=4,'yl'=2,'xh'=2,'xl'=2,'yh'=2,'core'=2] {'zr','yl','xh'..., dimensions={0} | all-to-all | bytes 294912 | tf_op jit(solution)/shard_map/all_to_all | solution.py:33
  78.7 0.6 copy-done.7
  79.6 0.6 copy-done.10
  80.7 15.9 %all_to_all.49 = bf16[128,2,144]{2,1,0:T(2,128)(2,1)S(1)} all-to-all(bf16[128,2,144]{2,1,0:T(2,128)(2,1)S(1)} %copy.46), channel_id=1, replica_groups=mesh['zq'=4,'zr'=4,'yl'=2,'xh'=2,'xl'=2,'yh'=2,'core'=2] {'zr','yl','xh'..., dimensions={0} | all-to-all | bytes 147456 | tf_op jit(solution)/shard_map/all_to_all | solution.py:33
  97.3 1.0 convolution_convert_fusion
  98.3 6.5 %all-to-all-start.3 = ((bf16[4,96,384]{2,1,0:T(8,128)(2,1)}), bf16[4,96,384]{2,1,0:T(8,128)(2,1)S(1)}, u32[]{:S(2)}, u32[]{:S(2)}) async-start(bf16[4,96,384]{2,1,0:T(8,128)(2,1)} %bitcast.15), calls=%async_computation.3 | async-start | bytes 589824 | tf_op jit(solution)/shard_map/all_to_all | solution.py:33
  104.8 0.8 fusion.13
  105.9 0.5 reshape.140
  106.9 15.3 %all-to-all-done.3 = bf16[4,96,384]{2,1,0:T(8,128)(2,1)S(1)} async-done(((bf16[4,96,384]{2,1,0:T(8,128)(2,1)}), bf16[4,96,384]{2,1,0:T(8,128)(2,1)S(1)}, u32[]{:S(2)}, u32[]{:S(2)}) %all-to-all-start.3) | async-done | bytes 294944 | tf_op jit(solution)/shard_map/all_to_all | solution.py:33
  123.4 0.9 copy.51
  124.2 10.2 %all-to-all-start.4 = ((bf16[128,2,288]{2,1,0:T(2,128)(2,1)}), bf16[128,2,288]{2,1,0:T(2,128)(2,1)S(1)}, u32[]{:S(2)}, u32[]{:S(2)}) async-start(bf16[128,2,288]{2,1,0:T(2,128)(2,1)} %copy.51), calls=%async_computation.4 | async-start | bytes 393216 | tf_op jit(solution)/shard_map/all_to_all | solution.py:33
  135.1 11.1 %all-to-all-done.4 = bf16[128,2,288]{2,1,0:T(2,128)(2,1)S(1)} async-done(((bf16[128,2,288]{2,1,0:T(2,128)(2,1)}), bf16[128,2,288]{2,1,0:T(2,128)(2,1)S(1)}, u32[]{:S(2)}, u32[]{:S(2)}) %all-to-all-start.4) | async-done | bytes 147488 | tf_op jit(solution)/shard_map/all_to_all | solution.py:33
  147.9 0.5 concatenate.11
  148.4 14.4 %all_to_all.50 = bf16[64,16,128]{2,1,0:T(8,128)(2,1)S(1)} all-to-all(bf16[64,16,128]{2,1,0:T(8,128)(2,1)S(1)} %bitcast.124), channel_id=1, replica_groups=mesh['zq'=4,'zr'=4,'yl'=2,'xh'=2,'xl'=2,'yh'=2,'core'=2] {'zr','yl','xh'..., dimensions={0} | all-to-all | bytes 524288 | tf_op jit(solution)/shard_map/all_to_all | solution.py:33
  162.8 19.1 %all_to_all.51 = f32[8,16,128]{2,1,0:T(8,128)S(1)} all-to-all(f32[8,16,128]{2,1,0:T(8,128)S(1)} %broadcast_in_dim.7), channel_id=1, replica_groups=mesh['zq'=4,'zr'=4,'yl'=2,'xh'=2,'xl'=2,'yh'=2,'core'=2] {'zq','core'}, dimensions={0} | all-to-all | bytes 131072 | tf_op jit(solution)/shard_map/all_to_all | solution.py:33
  182.0 0.7 broadcast_in_dim.8
  182.7 5.3 %all-to-all-start.7 = ((bf16[64,16,128]{2,1,0:T(8,128)(2,1)}), bf16[64,16,128]{2,1,0:T(8,128)(2,1)S(1)}, u32[]{:S(2)}, u32[]{:S(2)}) async-start(bf16[64,16,128]{2,1,0:T(8,128)(2,1)} %broadcast_in_dim.8), calls=%async_computation.7 | async-start | bytes 524288 | tf_op jit(solution)/shard_map/all_to_all | solution.py:33
  188.0 0.9 multiply_convert_fusion
  188.9 9.0 %all-to-all-done.7 = bf16[64,16,128]{2,1,0:T(8,128)(2,1)S(1)} async-done(((bf16[64,16,128]{2,1,0:T(8,128)(2,1)}), bf16[64,16,128]{2,1,0:T(8,128)(2,1)S(1)}, u32[]{:S(2)}, u32[]{:S(2)}) %all-to-all-start.7) | async-done | bytes 262176 | tf_op jit(solution)/shard_map/all_to_all | solution.py:33
  197.9 0.7 fusion.31
  198.6 0.6 slice.107
  199.2 0.7 copy-done.6
  (81 shorter events, 9.8 us)
Async XLA Ops:
  0.6 18.3 %copy-start = (bf16[128,128]{1,0:T(8,128)(2,1)S(1)}, bf16[128,128]{1,0:T(8,128)(2,1)}, u32[]{:S(2)}) copy-start(bf16[128,128]{1,0:T(8,128)(2,1)} %param.15) | copy-start | bytes 98308
  0.6 1.1 copy-start.1
  1.9 0.7 copy-start.8
  1.9 0.7 copy-start.9
  2.0 0.9 copy-start.2
  4.2 14.0 %copy-start.4 = (bf16[12,24,128]{2,1,0:T(8,128)(2,1)S(1)}, bf16[12,24,128]{2,1,0:T(8,128)(2,1)}, u32[]{:S(2)}) copy-start(bf16[12,24,128]{2,1,0:T(8,128)(2,1)} %param.9) | copy-start | bytes 221188
  4.2 25.7 %all-to-all-start = ((bf16[128,2,288]{2,1,0:T(2,128)(2,1)}), bf16[128,2,288]{2,1,0:T(2,128)(2,1)S(1)}, u32[]{:S(2)}, u32[]{:S(2)}) async-start(bf16[128,2,288]{2,1,0:T(2,128)(2,1)} %copy.40), calls=%async_computation | async-start | bytes 393216 | tf_op jit(solution)/shard_map/all_to_all | solution.py:33
  78.7 0.7 copy-start.7
  79.6 0.7 copy-start.10
  98.3 6.5 %copy-start.3 = (f32[288,128]{1,0:T(8,128)S(1)}, f32[288,128]{1,0:T(8,128)}, u32[]{:S(2)}) copy-start(f32[288,128]{1,0:T(8,128)} %get-tuple-element.40) | copy-start | bytes 442372
  98.3 6.5 %copy-start.5 = (bf16[12,24,128]{2,1,0:T(8,128)(2,1)S(1)}, bf16[12,24,128]{2,1,0:T(8,128)(2,1)}, u32[]{:S(2)}) copy-start(bf16[12,24,128]{2,1,0:T(8,128)(2,1)} %param.9) | copy-start | bytes 221188
  98.3 23.9 %all-to-all-start.3 = ((bf16[4,96,384]{2,1,0:T(8,128)(2,1)}), bf16[4,96,384]{2,1,0:T(8,128)(2,1)S(1)}, u32[]{:S(2)}, u32[]{:S(2)}) async-start(bf16[4,96,384]{2,1,0:T(8,128)(2,1)} %bitcast.15), calls=%async_computation.3 | async-start | bytes 589824 | tf_op jit(solution)/shard_map/all_to_all | solution.py:33
  124.2 21.9 %all-to-all-start.4 = ((bf16[128,2,288]{2,1,0:T(2,128)(2,1)}), bf16[128,2,288]{2,1,0:T(2,128)(2,1)S(1)}, u32[]{:S(2)}, u32[]{:S(2)}) async-start(bf16[128,2,288]{2,1,0:T(2,128)(2,1)} %copy.51), calls=%async_computation.4 | async-start | bytes 393216 | tf_op jit(solution)/shard_map/all_to_all | solution.py:33
  182.7 15.1 %all-to-all-start.7 = ((bf16[64,16,128]{2,1,0:T(8,128)(2,1)}), bf16[64,16,128]{2,1,0:T(8,128)(2,1)S(1)}, u32[]{:S(2)}, u32[]{:S(2)}) async-start(bf16[64,16,128]{2,1,0:T(8,128)(2,1)} %broadcast_in_dim.8), calls=%async_computation.7 | async-start | bytes 524288 | tf_op jit(solution)/shard_map/all_to_all | solution.py:33
  199.2 0.7 copy-start.6
